TPU v7x, 128 devices: a whole 4x4x4 slice. The times are simulated.
128 devices in a mesh: grp: 16 (over x, z), sp: 8 (over y, core).
Axes of the slice: x: 4, y: 4, z: 4, core: 2. Of those that a mesh axis runs over, the one named last changes fastest.
Arguments:
- queries: bfloat16 [20480, 4096], P(('grp', 'sp')), may hold values from -128 to 128
- fresh_key_values: bfloat16 [20480, 1024], P(('grp', 'sp')), may hold values from -4 to 4
- cache: bfloat16 [16, 8, 256, 256], P('grp', 'sp'), may hold values from -4 to 4
- lengths: int32 [16, 8], P('grp', 'sp'), may hold values from 1 to 160, 1024 in all within a row
- out_weight: bfloat16 [4096, 2048], P('sp'), may hold values from -1 to 1
- residual: bfloat16 [20480, 2048], P(('grp', 'sp')), may hold values from -36 to 36
- norm_gain: float32 [2048], replicated, may hold values from 0.1 to 1.9
- expert_ids: int32 [20480, 8], P(('grp', 'sp')), may hold values from 0 to 127, all different within a row; in each aligned block of 160 rows (0 to 159, 160 to 319, ...) at most 16 rows name the same one
- gate_values: float32 [20480, 8], P(('grp', 'sp')), may hold values from 0.05 to 0.5
- up_gate_weight: bfloat16 [128, 2048, 1536], P(('grp', 'sp')), may hold values from -0.125 to 0.125
- down_weight: bfloat16 [128, 768, 2048], P(('grp', 'sp')), may hold values from -0.21875 to 0.21875
Outputs:
- attended: bfloat16 [20480, 2048], P(('grp', 'sp'))
- moe_out: bfloat16 [20480, 2048], P(('grp', 'sp'))
Inputs may be any that keep to these rules, and one draw needn't show every extreme that they name: Each group's 8 lengths sum to 1024, and in every group one device has exactly 160. `expert_ids`: each slot names 8 different experts; among the 160 slots of one device no expert is named more than 16 times, and one expert is named exactly 16 times by the slots of some device.
All inputs are finite; a program needn't handle non-finite values.
Results may differ from a plain program's by a relative error of at most 0.02.
Values may be sent and summed in bfloat16 or wider, within the bound.
A program may use at most 128 MiB of HBM per device.

v0:
```python
import math

import jax
import jax.numpy as jnp
from jax import lax
from jax.sharding import PartitionSpec as P


def from_everyone(x, axis):
    devices = lax.axis_size(axis)
    return lax.all_to_all(jnp.broadcast_to(x[None], (devices, *x.shape)), axis, 0, 0, tiled=True)


def in_order(pieces, dim):
    shape = list(pieces.shape[1:])
    shape[dim] *= pieces.shape[0]
    return jnp.moveaxis(pieces, 0, dim).reshape(shape)


def gather_directly(x, axis, dim):
    pieces = from_everyone(x, axis)
    return in_order(pieces, dim)


def partner_2(value, axis, bit):
    mask = 2**bit
    pairs = [(source, source ^ mask) for source in range(lax.axis_size(axis))]
    return lax.ppermute(value, axis, pairs)


def split_up(x, dim, devices):
    before, after = (x.shape[:dim], x.shape[dim + 1 :])
    return jnp.moveaxis(x.reshape(*before, devices, -1, *after), dim, 0)


def exchange_both(x, axis, axes, splits, concats):
    sizes = [lax.axis_size(a) for a in axes]
    pieces = split_up(x, splits[0], sizes[0])
    pieces = jnp.moveaxis(split_up(pieces, splits[1] + 1, sizes[1]), 0, 1)
    inside = pieces.shape[2:]
    pieces = pieces.reshape(-1, *inside)
    pieces = lax.all_to_all(pieces, axis, split_axis=0, concat_axis=0, tiled=True)
    pieces = in_order(pieces.reshape(*sizes, *inside), concats[0] + 1)
    return in_order(pieces, concats[1])


def per_device(
    queries,
    fresh_key_values,
    cache,
    lengths,
    out_weight,
    residual,
    norm_gain,
    expert_ids,
    gate_values,
    up_gate_weight,
    down_weight,
):
    seq_devices = lax.axis_size("sp")
    slot_rows = queries.shape[0]
    head_width = cache.shape[-1] // 2
    model_width = residual.shape[1]
    kv_heads = fresh_key_values.shape[1] // (2 * head_width)
    repeat = seq_devices // kv_heads
    keys_new = fresh_key_values[:, : kv_heads * head_width].reshape(
        slot_rows, kv_heads, 1, head_width
    )
    values_new = fresh_key_values[:, kv_heads * head_width :].reshape(
        slot_rows, kv_heads, 1, head_width
    )
    paired = jnp.concatenate([keys_new, values_new], axis=3)
    spread = jnp.broadcast_to(paired, (slot_rows, kv_heads, repeat, 2 * head_width)).reshape(
        slot_rows, seq_devices * 2 * head_width
    )
    all_lengths = gather_directly(lengths, "sp", 1)
    queries_by_head, head_kv = (
        lax.all_to_all(queries, "sp", split_axis=1, concat_axis=0, tiled=True),
        lax.all_to_all(spread, "sp", split_axis=1, concat_axis=0, tiled=True),
    )
    cache_block = cache[0, 0]
    my_index = lax.axis_index("sp")
    partner = partner_2(cache_block, "sp", 0)
    is_upper = my_index // 2**0 % 2 == 1
    cache_block = jnp.where(
        is_upper,
        jnp.concatenate([partner, cache_block], axis=0),
        jnp.concatenate([cache_block, partner], axis=0),
    )
    stretch_lens = all_lengths[0]
    offsets = jnp.cumsum(stretch_lens) - stretch_lens
    rows_of_group = queries_by_head.shape[0]
    slot_ids = jnp.arange(rows_of_group, dtype=jnp.int32)
    source = slot_ids // slot_rows
    within = slot_ids % slot_rows
    from_device = source[:, None] == jnp.arange(seq_devices, dtype=jnp.int32)[None, :]
    is_live = within < jnp.sum(jnp.where(from_device, stretch_lens[None, :], 0), axis=1)
    position = within + jnp.sum(jnp.where(from_device, offsets[None, :], 0), axis=1)
    per_dev = queries_by_head.shape[1] // head_width
    cache_len = cache_block.shape[0]
    key_all = jnp.concatenate([cache_block[:, :head_width], head_kv[:, :head_width]], axis=0)
    value_all = jnp.concatenate([cache_block[:, head_width:], head_kv[:, head_width:]], axis=0)
    block_count = 2
    block_rows = rows_of_group // block_count

    def attend(parts):
        query_block, place_block = parts
        scores = jnp.einsum(
            "rhd,kd->hrk", query_block, key_all, preferred_element_type=jnp.float32
        ) / math.sqrt(head_width)
        allowed = jnp.concatenate(
            [
                jnp.ones((block_rows, cache_len), dtype=bool),
                is_live[None, :] & (position[None, :] <= place_block[:, None]),
            ],
            axis=1,
        )
        scores = jnp.where(allowed[None], scores, -jnp.inf)
        row_max = jnp.max(scores, axis=-1, keepdims=True)
        weights = jnp.exp(scores - row_max)
        totals = jnp.sum(weights, axis=-1, keepdims=True)
        result = (
            jnp.einsum(
                "hrk,kd->hrd",
                weights.astype(jnp.bfloat16),
                value_all,
                preferred_element_type=jnp.float32,
            )
            / totals
        )
        return (
            result.astype(jnp.bfloat16).transpose(1, 0, 2).reshape(block_rows, per_dev * head_width)
        )

    attn_heads = lax.map(
        attend,
        (
            queries_by_head.reshape(block_count, block_rows, per_dev, head_width),
            position.reshape(block_count, block_rows),
        ),
    ).reshape(rows_of_group, per_dev * head_width)
    attn_sum = lax.psum_scatter(
        jnp.dot(attn_heads, out_weight, preferred_element_type=jnp.float32).astype(jnp.bfloat16),
        "sp",
        scatter_dimension=0,
        tiled=True,
    ).astype(jnp.float32)
    own_live = jnp.arange(slot_rows, dtype=jnp.int32) < lengths[0, 0]
    attended = jnp.where(own_live[:, None], attn_sum, 0.0).astype(jnp.bfloat16)
    mixed_rows = residual.astype(jnp.float32) + attn_sum
    normed = (
        mixed_rows
        * lax.rsqrt(jnp.mean(mixed_rows * mixed_rows, axis=-1, keepdims=True) + 1e-06)
        * norm_gain
    ).astype(jnp.bfloat16)
    group_count = lax.axis_size("grp")
    experts = up_gate_weight.shape[0] * group_count * seq_devices
    top_count = expert_ids.shape[1]
    capacity = max(2, 8 * slot_rows * top_count // (5 * experts))
    hidden_width = down_weight.shape[1]
    choose = expert_ids[:, :, None] == jnp.arange(experts, dtype=jnp.int32)[None, None, :]
    routed = (jnp.any(choose, axis=1) & own_live[:, None]).astype(jnp.float32)
    earlier = (jnp.arange(slot_rows)[:, None] > jnp.arange(slot_rows)[None, :]).astype(jnp.float32)
    prefix = jnp.dot(earlier, routed, precision=lax.Precision.HIGHEST)
    slot_in = jnp.sum(jnp.where(choose, prefix[:, None, :], 0.0), axis=2).astype(jnp.int32)
    dump_slot = experts * capacity
    target = jnp.where(own_live[:, None], expert_ids * capacity + slot_in, dump_slot)
    slot_range = jnp.arange(dump_slot, dtype=jnp.int32)
    hits = target.T[:, None, :] == slot_range[None, :, None]
    select = jnp.any(hits, axis=0).astype(jnp.bfloat16)
    outgoing = jnp.dot(select, normed, preferred_element_type=jnp.float32).astype(jnp.bfloat16)
    sectioned = outgoing.reshape(group_count, seq_devices, capacity, model_width)
    arrived = exchange_both(sectioned, ("grp", "sp"), ("grp", "sp"), (0, 1), (0, 1))
    flat_rows = arrived.reshape(-1, model_width)
    projected = jnp.dot(flat_rows, up_gate_weight[0], preferred_element_type=jnp.float32)
    hidden = (jax.nn.silu(projected[:, :hidden_width]) * projected[:, hidden_width:]).astype(
        jnp.bfloat16
    )
    returned = exchange_both(
        jnp.dot(hidden, down_weight[0], preferred_element_type=jnp.float32)
        .astype(jnp.bfloat16)
        .reshape(arrived.shape),
        ("grp", "sp"),
        ("grp", "sp"),
        (0, 1),
        (0, 1),
    )
    matches = target[:, :, None] == slot_range[None, None, :]
    mixing = jnp.sum(jnp.where(matches, gate_values[:, :, None], 0.0), axis=1)
    combined = jnp.dot(
        mixing.astype(jnp.bfloat16),
        returned.reshape(dump_slot, model_width),
        preferred_element_type=jnp.float32,
    )
    moe_out = jnp.where(own_live[:, None], combined, 0.0).astype(jnp.bfloat16)
    return (attended, moe_out)


def solution(mesh):
    in_specs = (
        P(("grp", "sp"), None),
        P(("grp", "sp"), None),
        P("grp", "sp", None, None),
        P("grp", "sp"),
        P("sp", None),
        P(("grp", "sp"), None),
        P(),
        P(("grp", "sp"), None),
        P(("grp", "sp"), None),
        P(("grp", "sp"), None, None),
        P(("grp", "sp"), None, None),
    )
    out_specs = (P(("grp", "sp"), None), P(("grp", "sp"), None))
    return jax.shard_map(
        per_device, mesh=mesh, in_specs=in_specs, out_specs=out_specs, check_vma=False
    )
```

profile of v0, /device:TPU:1, one launch (start us, length us, event | category | flops | bytes accessed | tf_op | source)
XLA Modules:
  0.0 427.7 jit_solution(18035659371543107738)
XLA Ops:
  9.9 4.9 %all-to-all-start = ((s32[8,1,1]{2,1,0:T(1,128)}), s32[8,1,1]{2,1,0:T(1,128)S(1)}, u32[]{:S(2)}, u32[]{:S(2)}) async-start(s32[8,1,1]{2,1,0:T(1,128)} %broadcast_in_dim.129), calls=%async_computation | async-start | bytes 8192 | tf_op jit(solution)/shard_map/all_to_all | solution.py:11
  22.6 4.8 %all-to-all-start.2 = ((bf16[160,8,256]{2,0,1:T(8,128)(2,1)}), bf16[160,8,256]{2,0,1:T(8,128)(2,1)}, u32[]{:S(2)}, u32[]{:S(2)}) async-start(bf16[160,8,256]{2,0,1:T(8,128)(2,1)} %bitcast.112), calls=%async_computation.2 | async-start | bytes 1310720 | tf_op jit(solution)/shard_map/all_to_all | solution.py:79
  28.0 10.3 %all-to-all-done.2 = bf16[160,8,256]{2,0,1:T(8,128)(2,1)} async-done(((bf16[160,8,256]{2,0,1:T(8,128)(2,1)}), bf16[160,8,256]{2,0,1:T(8,128)(2,1)}, u32[]{:S(2)}, u32[]{:S(2)}) %all-to-all-start.2) | async-done | bytes 655392 | tf_op jit(solution)/shard_map/all_to_all | solution.py:79
  38.2 5.1 %all-to-all-start.1 = ((bf16[160,8,512]{2,0,1:T(8,128)(2,1)}), bf16[160,8,512]{2,0,1:T(8,128)(2,1)}, u32[]{:S(2)}, u32[]{:S(2)}) async-start(bf16[160,8,512]{2,0,1:T(8,128)(2,1)} %bitcast.111), calls=%async_computation.1 | async-start | bytes 2621440 | tf_op jit(solution)/shard_map/all_to_all | solution.py:78
  48.6 12.6 %all-to-all-done.1 = bf16[160,8,512]{2,0,1:T(8,128)(2,1)} async-done(((bf16[160,8,512]{2,0,1:T(8,128)(2,1)}), bf16[160,8,512]{2,0,1:T(8,128)(2,1)}, u32[]{:S(2)}, u32[]{:S(2)}) %all-to-all-start.1) | async-done | bytes 1310752 | tf_op jit(solution)/shard_map/all_to_all | solution.py:78
  61.2 3.6 reshape.121
  64.8 44.4 %while.10 = (s32[]{:T(128)}, bf16[2,640,512]{2,1,0:T(8,128)(2,1)}, pred[1280]{0:T(1024)(128)(4,1)S(1)}, s32[1280]{0:T(1024)S(1)}, s32[2,640]{1,0:T(2,128)S(1)}, ...) while((s32[]{:T(128)}, bf16[2,640,512]{2,1,0:T(8,128)(2,1)}, ...), condition=%wide.region_6.7_spmd, body=%wide.region_3.6_spmd.sunk | while | flops 2401561600 | bytes 69337480 | solution.py:135
  66.9 4.8 %bitcast_reduce_fusion.2 = (f32[4,640]{1,0:T(4,128)S(1)}, f32[640,4,1792]{2,0,1:T(8,128)S(1)}) fusion(pred[640,1792]{1,0:T(8,128)(4,1)S(1)} %concatenate.24, bf16[1792,128]{1,0:T(8,128)(2,1)} %get-tuple-element.202, bf16[1,640,4,128]{3,2,1,0:T(4,128)(2,1)S(1)} %constant_dynamic-slice_fusion.2), kind=kOutput, calls=%fused_computation.1.clone.1 | convolution fusion | flops 1188165120 | bytes 20621312 | tf_op jit(solution)/shard_map/while/body/eval_jaxpr/rhd,kd->hrk/dot_general | solution.py:108
  71.7 4.9 %fusion.55 = f32[4,640]{1,0:T(4,128)S(1)} fusion(f32[640,4,1792]{2,0,1:T(8,128)S(1)} %get-tuple-element.174, f32[4,640]{1,0:T(4,128)S(1)} %get-tuple-element.175, pred[640,1792]{1,0:T(8,128)(4,1)S(1)} %concatenate.24), kind=kLoop, calls=%fused_computation.4.clone.1 | loop fusion | flops 18347520 | bytes 19517440 | tf_op jit(solution)/shard_map/while/body/eval_jaxpr/reduce_sum | solution.py:121
  76.6 6.3 %divide_convert_fusion.2 = bf16[640,4,128]{0,2,1:T(8,128)(2,1)} fusion(f32[640,4,1792]{2,0,1:T(8,128)S(1)} %get-tuple-element.174, f32[4,640]{1,0:T(4,128)S(1)} %get-tuple-element.175, pred[640,1792]{1,0:T(8,128)(4,1)S(1)} %concatenate.24, f32[640,4]{0,1:T(4,128)S(1)} %bitcast.114, bf16[1792,128]{0,1:T(8,128)(2,1)S(1)} %copy-done.1), kind=kOutput, calls=%fused_computation.10.clone.1 | convolution fusion | flops 1193410560 | bytes 20631552 | tf_op jit(solution)/shard_map/while/body/eval_jaxpr/hrk,kd->hrd/dot_general | solution.py:123
  89.2 4.7 %bitcast_reduce_fusion.2 = (f32[4,640]{1,0:T(4,128)S(1)}, f32[640,4,1792]{2,0,1:T(8,128)S(1)}) fusion(pred[640,1792]{1,0:T(8,128)(4,1)S(1)} %concatenate.24, bf16[1792,128]{1,0:T(8,128)(2,1)} %get-tuple-element.202, bf16[1,640,4,128]{3,2,1,0:T(4,128)(2,1)S(1)} %constant_dynamic-slice_fusion.2), kind=kOutput, calls=%fused_computation.1.clone.1 | convolution fusion | flops 1188165120 | bytes 20621312 | tf_op jit(solution)/shard_map/while/body/eval_jaxpr/rhd,kd->hrk/dot_general | solution.py:108
  93.9 4.9 %fusion.55 = f32[4,640]{1,0:T(4,128)S(1)} fusion(f32[640,4,1792]{2,0,1:T(8,128)S(1)} %get-tuple-element.174, f32[4,640]{1,0:T(4,128)S(1)} %get-tuple-element.175, pred[640,1792]{1,0:T(8,128)(4,1)S(1)} %concatenate.24), kind=kLoop, calls=%fused_computation.4.clone.1 | loop fusion | flops 18347520 | bytes 19517440 | tf_op jit(solution)/shard_map/while/body/eval_jaxpr/reduce_sum | solution.py:121
  98.8 6.3 %divide_convert_fusion.2 = bf16[640,4,128]{0,2,1:T(8,128)(2,1)} fusion(f32[640,4,1792]{2,0,1:T(8,128)S(1)} %get-tuple-element.174, f32[4,640]{1,0:T(4,128)S(1)} %get-tuple-element.175, pred[640,1792]{1,0:T(8,128)(4,1)S(1)} %concatenate.24, f32[640,4]{0,1:T(4,128)S(1)} %bitcast.114, bf16[1792,128]{0,1:T(8,128)(2,1)S(1)} %copy-done.1), kind=kOutput, calls=%fused_computation.10.clone.1 | convolution fusion | flops 1193410560 | bytes 20631552 | tf_op jit(solution)/shard_map/while/body/eval_jaxpr/hrk,kd->hrd/dot_general | solution.py:123
  109.2 7.2 %convolution_convert_fusion = bf16[1280,2048]{1,0:T(8,128)(2,1)} fusion(bf16[1280,512]{1,0:T(8,128)(2,1)} %bitcast.121, bf16[512,2048]{1,0:T(8,128)(2,1)} %param.17), kind=kOutput, calls=%fused_computation.24 | convolution fusion | flops 2686976000 | bytes 8650752 | tf_op jit(solution)/shard_map/dot_general | solution.py:143
  119.5 35.2 %reduce-scatter.2.cloned.1.call-done = bf16[160,2048]{1,0:T(8,128)(2,1)} async-done(((bf16[1280,2048]{1,0:T(8,128)(2,1)}), bf16[160,2048]{1,0:T(8,128)(2,1)}) %reduce-scatter.2.cloned.1.call-update) | async-done | bytes 655376 | tf_op jit(solution)/shard_map/reduce_scatter | solution.py:142
  154.7 2.5 multiply_reduce_fusion
  157.3 3.9 convolution_convert_fusion.2
  161.2 108.2 %all_to_all.50 = bf16[128,1,1,16,2048]{4,3,2,1,0:T(8,128)(2,1)S(1)} all-to-all(bf16[128,1,1,16,2048]{4,3,2,1,0:T(8,128)(2,1)S(1)} %bitcast.107), channel_id=1, replica_groups=mesh['grp'=16,'sp'=8] {'grp','sp'}, dimensions={0} | all-to-all | bytes 16777216 | tf_op jit(solution)/shard_map/all_to_all | solution.py:42
  269.4 15.7 %fusion.18 = f32[2048,1536]{1,0:T(8,128)} fusion(bf16[2048,2048]{1,0:T(8,128)(2,1)S(1)} %bitcast.110, bf16[1,2048,1536]{2,1,0:T(8,128)(2,1)S(1)} %bitcast.120), kind=kOutput, calls=%fused_computation.29 | convolution fusion | flops 12884901888 | bytes 27262976 | tf_op jit(solution)/shard_map/dot_general | solution.py:175
  285.1 13.9 %convolution_convert_fusion.1 = bf16[2048,2048]{1,0:T(8,128)(2,1)} fusion(f32[2048,1536]{1,0:T(8,128)} %fusion.18, bf16[1,768,2048]{2,1,0:T(8,128)(2,1)S(1)} %copy-done), kind=kOutput, calls=%fused_computation.25 | convolution fusion | flops 6456082432 | bytes 24117248 | tf_op jit(solution)/shard_map/dot_general | solution.py:180
  299.0 9.7 %all-to-all-start.4 = ((bf16[128,1,1,16,2048]{4,3,2,1,0:T(8,128)(2,1)}), bf16[128,1,1,16,2048]{4,3,2,1,0:T(8,128)(2,1)}, u32[]{:S(2)}, u32[]{:S(2)}) async-start(bf16[128,1,1,16,2048]{4,3,2,1,0:T(8,128)(2,1)} %bitcast.109), calls=%async_computation.5 | async-start | bytes 16777216 | tf_op jit(solution)/shard_map/all_to_all | solution.py:42
  309.0 4.4 %select_reduce_fusion = bf16[160,2048]{1,0:T(8,128)(2,1)} fusion(f32[160,8]{1,0:T(8,128)S(1)} %copy.72, s32[160,8]{1,0:T(8,128)S(1)} %copy.71), kind=kLoop, calls=%fused_computation.21 | loop fusion | flops 7536640 | bytes 665600 | tf_op jit(solution)/shard_map/reduce_sum | solution.py:189
  313.3 101.6 %all-to-all-done.4 = bf16[128,1,1,16,2048]{4,3,2,1,0:T(8,128)(2,1)} async-done(((bf16[128,1,1,16,2048]{4,3,2,1,0:T(8,128)(2,1)}), bf16[128,1,1,16,2048]{4,3,2,1,0:T(8,128)(2,1)}, u32[]{:S(2)}, u32[]{:S(2)}) %all-to-all-start.4) | async-done | bytes 8388640 | tf_op jit(solution)/shard_map/all_to_all | solution.py:42
  414.9 6.0 %fusion.23 = bf16[160,2048]{1,0:T(8,128)(2,1)} fusion(bf16[2048,2048]{1,0:T(8,128)(2,1)} %bitcast.33, bf16[160,2048]{1,0:T(8,128)(2,1)} %select_reduce_fusion, pred[160]{0:T(512)(128)(4,1)S(1)} %iota_compare_fusion.6), kind=kOutput, calls=%fused_computation.34 | convolution fusion | flops 1342832640 | bytes 9699488 | tf_op jit(solution)/shard_map/dot_general | solution.py:190
  (69 shorter events, 31.4 us)
Async XLA Ops:
  7.2 277.9 %copy-start = (bf16[1,768,2048]{2,1,0:T(8,128)(2,1)S(1)}, bf16[1,768,2048]{2,1,0:T(8,128)(2,1)}, u32[]{:S(2)}) copy-start(bf16[1,768,2048]{2,1,0:T(8,128)(2,1)} %param.23) | copy-start | bytes 9437188
  7.2 36.2 %collective-permute-start = (bf16[256,256]{1,0:T(8,128)(2,1)}, bf16[256,256]{1,0:T(8,128)(2,1)}, u32[]{:S(2)}, u32[]{:S(2)}) collective-permute-start(bf16[256,256]{1,0:T(8,128)(2,1)} %bitcast.115), channel_id=1, source_target_pairs={{0,1},{1,0},{2,3},{3,2},{4,5},{5,4},{6,7},{7,6},{8,9},{9,8},{10,11... | collective-permute-start | bytes 393224 | tf_op jit(solution)/shard_map/ppermute | solution.py:28
  9.9 11.8 %all-to-all-start = ((s32[8,1,1]{2,1,0:T(1,128)}), s32[8,1,1]{2,1,0:T(1,128)S(1)}, u32[]{:S(2)}, u32[]{:S(2)}) async-start(s32[8,1,1]{2,1,0:T(1,128)} %broadcast_in_dim.129), calls=%async_computation | async-start | bytes 8192 | tf_op jit(solution)/shard_map/all_to_all | solution.py:11
  22.6 15.7 %all-to-all-start.2 = ((bf16[160,8,256]{2,0,1:T(8,128)(2,1)}), bf16[160,8,256]{2,0,1:T(8,128)(2,1)}, u32[]{:S(2)}, u32[]{:S(2)}) async-start(bf16[160,8,256]{2,0,1:T(8,128)(2,1)} %bitcast.112), calls=%async_computation.2 | async-start | bytes 1310720 | tf_op jit(solution)/shard_map/all_to_all | solution.py:79
  38.2 23.0 %all-to-all-start.1 = ((bf16[160,8,512]{2,0,1:T(8,128)(2,1)}), bf16[160,8,512]{2,0,1:T(8,128)(2,1)}, u32[]{:S(2)}, u32[]{:S(2)}) async-start(bf16[160,8,512]{2,0,1:T(8,128)(2,1)} %bitcast.111), calls=%async_computation.1 | async-start | bytes 2621440 | tf_op jit(solution)/shard_map/all_to_all | solution.py:78
  43.3 111.4 %reduce-scatter.2.cloned.1.call-start = ((), (), s32[]{:S(2)}) async-start(), calls=%async_computation.6 | async-start | bytes 5898240 | tf_op jit(solution)/shard_map/reduce_scatter | solution.py:142
  71.7 4.9 %copy-start.1 = (bf16[1792,128]{0,1:T(8,128)(2,1)S(1)}, bf16[1792,128]{0,1:T(8,128)(2,1)}, u32[]{:S(2)}) copy-start(bf16[1792,128]{0,1:T(8,128)(2,1)} %get-tuple-element.203) | copy-start | bytes 1376260 | tf_op jit(solution)/shard_map/while
  93.9 4.9 %copy-start.1 = (bf16[1792,128]{0,1:T(8,128)(2,1)S(1)}, bf16[1792,128]{0,1:T(8,128)(2,1)}, u32[]{:S(2)}) copy-start(bf16[1792,128]{0,1:T(8,128)(2,1)} %get-tuple-element.203) | copy-start | bytes 1376260 | tf_op jit(solution)/shard_map/while
  109.2 7.2 %copy-start.2 = (s32[160,8]{0,1:T(8,128)S(1)}, s32[160,8]{0,1:T(8,128)}, u32[]{:S(2)}) copy-start(s32[160,8]{0,1:T(8,128)} %param.20) | copy-start | bytes 15364
  116.4 40.8 %copy-start.3 = (f32[2048]{0:T(1024)S(1)}, f32[2048]{0:T(1024)}, u32[]{:S(2)}) copy-start(f32[2048]{0:T(1024)} %param.19) | copy-start | bytes 24580
  157.3 112.1 %slice-start = ((s8[6291456]{0:T(1024)(128)(4,1)}), s8[4194304]{0:T(1024)(128)(4,1)S(1)}, s32[]{:S(2)}) async-start(s8[6291456]{0:T(1024)(128)(4,1)} %bitcast.119), calls=%async_computation.7 | async-start | bytes 8388608
  161.2 108.2 %slice-start.1 = ((s8[6291456]{0:T(1024)(128)(4,1)}), s8[2097152]{0:T(1024)(128)(4,1)S(1)}, s32[]{:S(2)}) async-start(s8[6291456]{0:T(1024)(128)(4,1)} %bitcast.119), calls=%async_computation.8 | async-start | bytes 4194304
  299.0 9.9 %copy-start.4 = (f32[160,8]{0,1:T(8,128)S(1)}, f32[160,8]{0,1:T(8,128)}, u32[]{:S(2)}) copy-start(f32[160,8]{0,1:T(8,128)} %param.21) | copy-start | bytes 15364
  299.0 115.9 %all-to-all-start.4 = ((bf16[128,1,1,16,2048]{4,3,2,1,0:T(8,128)(2,1)}), bf16[128,1,1,16,2048]{4,3,2,1,0:T(8,128)(2,1)}, u32[]{:S(2)}, u32[]{:S(2)}) async-start(bf16[128,1,1,16,2048]{4,3,2,1,0:T(8,128)(2,1)} %bitcast.109), calls=%async_computation.5 | async-start | bytes 16777216 | tf_op jit(solution)/shard_map/all_to_all | solution.py:42
Sparse Core Ops, SparseCore 0:
  116.6 38.1 reduce-scatter.1
where the time goes:
time: 429 us; the launch traced here: 428 us
  waiting for transfers between devices  160 us (37%)
  blocking collectives  108 us (25%)
  matrix products  69 us (16%)
  starting transfers between devices  26 us (6%)
  local copies, waits for them, and re-layouts  25.7 us (6%)
  other arithmetic  24.2 us (6%)
  between operations  14.9 us (3%)
    all_to_all x1, blocking collectives, exchange_both(): lax.all_to_all(pieces, axis, split_axis=0, concat_axis=0, tiled=True)  108 us
    all_to_all x1, waiting for transfers between devices, exchange_both(): lax.all_to_all(pieces, axis, split_axis=0, concat_axis=0, tiled=True)  102 us
    reduce_scatter x1, waiting for transfers between devices, per_device(): lax.psum_scatter(jnp.dot(attn_heads, out_weight, preferred_element_type=j...  35.2 us
    dot_general x1, matrix products, per_device(): jnp.dot(flat_rows, up_gate_weight[0], preferred_element_type=jnp.float32)  15.7 us
    dot_general x1, matrix products, per_device(): jnp.dot(hidden, down_weight[0], preferred_element_type=jnp.float32)  13.9 us
    all_to_all x1, waiting for transfers between devices, per_device(): lax.all_to_all(queries, 'sp', split_axis=1, concat_axis=0, tiled=True)  12.6 us
    dot_general x2, matrix products, attend(): jnp.einsum('hrk,kd->hrd', weights.astype(jnp.bfloat16), value_all, prefer...  12.6 us
    all_to_all x1, waiting for transfers between devices, per_device(): lax.all_to_all(spread, 'sp', split_axis=1, concat_axis=0, tiled=True)  10.3 us
  transfers between devices with their start and end apart: 6, of which 4 were waited for; matrix products, arithmetic and copies ran while one was open for 5% of the time, Pallas kernels for 0%

commit v1 on v0

v1 whole, which is shorter than its diff:
```python
import functools
import math

import jax
import jax.numpy as jnp
from jax import lax
from jax.experimental import pallas as pl
from jax.experimental.pallas import tpu as pltpu
from jax.sharding import PartitionSpec as P


def in_order(pieces, dim):
    shape = list(pieces.shape[1:])
    shape[dim] *= pieces.shape[0]
    return jnp.moveaxis(pieces, 0, dim).reshape(shape)


def split_up(x, dim, devices):
    before, after = (x.shape[:dim], x.shape[dim + 1 :])
    return jnp.moveaxis(x.reshape(*before, devices, -1, *after), dim, 0)


def exchange_both(x, axis, axes, splits, concats):
    sizes = [lax.axis_size(a) for a in axes]
    pieces = split_up(x, splits[0], sizes[0])
    pieces = jnp.moveaxis(split_up(pieces, splits[1] + 1, sizes[1]), 0, 1)
    inside = pieces.shape[2:]
    pieces = pieces.reshape(-1, *inside)
    pieces = lax.all_to_all(pieces, axis, split_axis=0, concat_axis=0, tiled=True)
    pieces = in_order(pieces.reshape(*sizes, *inside), concats[0] + 1)
    return in_order(pieces, concats[1])


MESH = pl.DeviceIdType.MESH
NEG = -1e30


def group_attention(
    q_hbm, fkv_hbm, cache_hbm, lens_ref, w_hbm, res_hbm, gain_ref,
    attended_ref, normed_ref,
    qb, kx, vx, lb, w, res, heads, own_part, give, take, relay, half_in, full_in,
    q_send, k_send, v_send, l_send, q_recv, k_recv, v_recv, l_recv,
    c_send, c_recv, local, pair_send, pair_recv, ring_send, ring_recv,
):
    me = lax.axis_index("sp")
    devices = qb.shape[0]
    rows, wide = qb.shape[1], qb.shape[2]
    depth = kx.shape[1] // 2
    per = wide // depth
    block = cache_hbm.shape[0]
    cached = 2 * block
    chips = devices // 2
    y, c = me // 2, lax.rem(me, 2)
    partner = y * 2 + 1 - c
    width = w.shape[1]
    half = width // 2

    bar = pltpu.get_barrier_semaphore()
    for i in range(1, devices):
        pl.semaphore_signal(
            bar, inc=1, device_id={"sp": lax.rem(me + i, devices)}, device_id_type=MESH
        )

    local_copies = [
        pltpu.make_async_copy(w_hbm, w, local.at[0]),
        pltpu.make_async_copy(res_hbm, res, local.at[1]),
        pltpu.make_async_copy(
            cache_hbm.at[:, pl.ds(0, depth)],
            kx.at[pl.ds(c * block, block), pl.ds(0, depth)],
            local.at[2],
        ),
        pltpu.make_async_copy(
            cache_hbm.at[:, pl.ds(depth, depth)],
            vx.at[pl.ds(c * block, block), pl.ds(0, depth)],
            local.at[3],
        ),
        pltpu.make_async_copy(
            fkv_hbm.at[:, pl.ds(y * depth, depth)],
            kx.at[pl.ds(cached + me * rows, rows), pl.ds(0, depth)],
            local.at[4],
        ),
        pltpu.make_async_copy(
            fkv_hbm.at[:, pl.ds((chips + y) * depth, depth)],
            vx.at[pl.ds(cached + me * rows, rows), pl.ds(0, depth)],
            local.at[5],
        ),
        pltpu.make_async_copy(q_hbm.at[:, pl.ds(me * wide, wide)], qb.at[me], local.at[6]),
        pltpu.make_async_copy(lens_ref, lb.at[me], local.at[7]),
    ]
    for copy in local_copies:
        copy.start()

    vx[:, depth:] = jnp.ones((vx.shape[0], depth), jnp.bfloat16)
    kx[:cached, depth:] = jnp.zeros((cached, depth), jnp.bfloat16)

    pl.semaphore_wait(bar, devices - 1)

    def k_copy(i):
        p = lax.rem(me + i, devices)
        return pltpu.make_async_remote_copy(
            fkv_hbm.at[:, pl.ds((p // 2) * depth, depth)],
            kx.at[pl.ds(cached + me * rows, rows), pl.ds(0, depth)],
            k_send.at[i], k_recv.at[i], device_id={"sp": p}, device_id_type=MESH,
        )

    def v_copy(i):
        p = lax.rem(me + i, devices)
        return pltpu.make_async_remote_copy(
            fkv_hbm.at[:, pl.ds((chips + p // 2) * depth, depth)],
            vx.at[pl.ds(cached + me * rows, rows), pl.ds(0, depth)],
            v_send.at[i], v_recv.at[i], device_id={"sp": p}, device_id_type=MESH,
        )

    def l_copy(i):
        p = lax.rem(me + i, devices)
        return pltpu.make_async_remote_copy(
            lens_ref, lb.at[me], l_send.at[i], l_recv.at[i],
            device_id={"sp": p}, device_id_type=MESH,
        )

    def q_copy(p):
        return pltpu.make_async_remote_copy(
            q_hbm.at[:, pl.ds(p * wide, wide)], qb.at[me], q_send.at[p], q_recv.at[me],
            device_id={"sp": p}, device_id_type=MESH,
        )

    cache_copies = [
        pltpu.make_async_remote_copy(
            cache_hbm.at[:, pl.ds(d * depth, depth)],
            dst.at[pl.ds(c * block, block), pl.ds(0, depth)],
            c_send.at[d], c_recv.at[d], device_id={"sp": partner}, device_id_type=MESH,
        )
        for d, dst in enumerate((kx, vx))
    ]
    far_first = (4, 5, 3, 2, 6, 1, 7)
    for i in far_first:
        k_copy(i).start()
        v_copy(i).start()
        l_copy(i).start()
    for copy in cache_copies:
        copy.start()
    q_copy(partner).start()
    for dy in (2, 1, 3):
        for cc in range(2):
            q_copy(lax.rem(y + dy, chips) * 2 + cc).start()

    for copy in local_copies:
        copy.wait()
    for copy in cache_copies:
        copy.wait_recv()
    for i in range(1, devices):
        l_copy(i).wait_recv()
        k_copy(i).wait_recv()
        v_copy(i).wait_recv()
    row_ids = lax.broadcasted_iota(jnp.int32, (rows, depth), 0)
    for t in range(devices):
        alive = row_ids < lb[t, 0:1, :]
        kx[cached + t * rows : cached + (t + 1) * rows, depth:] = jnp.where(
            alive, 0.0, NEG
        ).astype(jnp.bfloat16)

    scale = math.log2(math.e) / math.sqrt(depth)
    pair_rows = 2 * rows
    lane = lax.broadcasted_iota(jnp.int32, (pair_rows, depth), 1)
    pick = jnp.where(lane == 0, 1.0, 0.0).astype(jnp.bfloat16)

    def attend(chip):
        keys = cached + (chip + 1) * pair_rows
        first = (cached + chip * pair_rows) // 128 * 128
        shift = cached + chip * pair_rows - first

        def head(h, carry):
            q = qb[2 * chip : 2 * chip + 2, :, pl.ds(pl.multiple_of(h * depth, depth), depth)]
            q = jnp.concatenate([q.reshape(pair_rows, depth), pick], axis=1)
            dims = (((1,), (1,)), ((), ()))
            sa = lax.dot_general(q, kx[:first, :], dims, preferred_element_type=jnp.float32)
            sb = lax.dot_general(q, kx[first:keys, :], dims, preferred_element_type=jnp.float32)
            i = lax.broadcasted_iota(jnp.int32, sb.shape, 0)
            j = lax.broadcasted_iota(jnp.int32, sb.shape, 1)
            sb = jnp.where(j - shift <= i, sb, NEG)
            top = jnp.maximum(
                jnp.max(sa, axis=1, keepdims=True), jnp.max(sb, axis=1, keepdims=True)
            )
            pa = jnp.exp2((sa - top) * scale).astype(jnp.bfloat16)
            pb = jnp.exp2((sb - top) * scale).astype(jnp.bfloat16)
            out = jnp.dot(pa, vx[:first, :], preferred_element_type=jnp.float32)
            out = out + jnp.dot(pb, vx[first:keys, :], preferred_element_type=jnp.float32)
            heads[:, pl.ds(pl.multiple_of(h * depth, depth), depth)] = (
                out[:, :depth] / out[:, depth:]
            ).astype(jnp.bfloat16)
            return carry

        lax.fori_loop(0, per, head, 0)

    def pair_copy(slot):
        return pltpu.make_async_remote_copy(
            give.at[slot], take.at[slot], pair_send.at[slot], pair_recv.at[slot],
            device_id={"sp": partner}, device_id_type=MESH,
        )

    up = lax.rem(y + 1, chips) * 2 + c
    down = lax.rem(y + chips - 1, chips) * 2 + c

    def ring_copy(n):
        src, dst, to = (
            (relay.at[0, :, pl.ds(0, half)], half_in.at[0], up),
            (relay.at[0, :, pl.ds(half, half)], half_in.at[1], down),
            (relay.at[1], full_in.at[0], up),
            (relay.at[2], full_in.at[1], down),
        )[n]
        return pltpu.make_async_remote_copy(
            src, dst, ring_send.at[n], ring_recv.at[n],
            device_id={"sp": to}, device_id_type=MESH,
        )

    def project(side, store):
        mine = heads[pl.ds(pl.multiple_of(side * rows, rows), rows), :]
        for n in range(4):
            cols = slice(n * (width // 4), (n + 1) * (width // 4))
            store(cols, jnp.dot(mine, w[:, cols], preferred_element_type=jnp.float32))

    def step(n, carry):
        dy = jnp.where(n == 3, 3, lax.rem(n * 2, 3))
        chip = lax.rem(y + dy, chips)

        @pl.when(n > 0)
        def _():
            for cc in range(2):
                t = chip * 2 + cc
                pltpu.make_async_copy(qb.at[t], qb.at[t], q_recv.at[t]).wait()

        @pl.when(n == 0)
        def _():
            pltpu.make_async_copy(qb.at[partner], qb.at[partner], q_recv.at[partner]).wait()

        lax.switch(chip, [functools.partial(attend, k) for k in range(chips)])

        def to_give(cols, value):
            give[n, :, cols] = value.astype(jnp.bfloat16)

        def to_own(cols, value):
            own_part[n, :, cols] = value

        project(1 - c, to_give)
        pair_copy(n).start()
        project(c, to_own)

        @pl.when(n == 1)
        def _():
            pair_copy(1).wait_recv()
            relay[0] = (own_part[1] + take[1].astype(jnp.float32)).astype(jnp.bfloat16)
            ring_copy(0).start()
            ring_copy(1).start()

        @pl.when(n == 2)
        def _():
            pair_copy(2).wait_recv()
            ring_copy(0).wait_recv()
            relay[1, :, :half] = (
                own_part[2, :, :half]
                + take[2, :, :half].astype(jnp.float32)
                + half_in[0].astype(jnp.float32)
            ).astype(jnp.bfloat16)
            relay[1, :, half:] = (
                own_part[2, :, half:] + take[2, :, half:].astype(jnp.float32)
            ).astype(jnp.bfloat16)
            ring_copy(2).start()

        @pl.when(n == 3)
        def _():
            pair_copy(3).wait_recv()
            ring_copy(1).wait_recv()
            relay[2, :, :half] = (
                own_part[3, :, :half] + take[3, :, :half].astype(jnp.float32)
            ).astype(jnp.bfloat16)
            relay[2, :, half:] = (
                own_part[3, :, half:]
                + take[3, :, half:].astype(jnp.float32)
                + half_in[1].astype(jnp.float32)
            ).astype(jnp.bfloat16)
            ring_copy(3).start()

        return carry

    lax.fori_loop(0, chips, step, 0)
    pair_copy(0).wait_recv()
    own_part[0] = own_part[0] + take[0].astype(jnp.float32)
    ring_copy(2).wait_recv()
    own_part[0] = own_part[0] + full_in[0].astype(jnp.float32)
    ring_copy(3).wait_recv()
    total = own_part[0] + full_in[1].astype(jnp.float32)
    alive = lax.broadcasted_iota(jnp.int32, (rows, 128), 0) < lens_ref[0:1, :]
    keep = jnp.max(jnp.where(alive, 1.0, 0.0), axis=1, keepdims=True)
    attended_ref[...] = jnp.where(keep > 0.0, total, 0.0).astype(jnp.bfloat16)
    mixed = res[...].astype(jnp.float32) + total
    power = jnp.mean(mixed * mixed, axis=1, keepdims=True)
    normed_ref[...] = (mixed * lax.rsqrt(power + 1e-06) * gain_ref[...]).astype(jnp.bfloat16)

    for i in range(1, devices):
        k_copy(i).wait_send()
        v_copy(i).wait_send()
        l_copy(i).wait_send()
        q_copy(lax.rem(me + i, devices)).wait_send()
    for copy in cache_copies:
        copy.wait_send()
    for n in range(4):
        pair_copy(n).wait_send()
        ring_copy(n).wait_send()


def attention(queries, fresh_key_values, cache, lengths, out_weight, residual, norm_gain):
    devices = lax.axis_size("sp")
    rows, wide = queries.shape[0], queries.shape[1] // devices
    block, depth = cache.shape[2], cache.shape[3] // 2
    width = residual.shape[1]
    keys = 2 * block + devices * rows
    any_spec = pl.BlockSpec(memory_space=pl.ANY)
    vmem = pl.BlockSpec(memory_space=pltpu.VMEM)
    dma = pltpu.SemaphoreType.DMA
    out = jax.ShapeDtypeStruct((rows, width), jnp.bfloat16)
    return pl.pallas_call(
        group_attention,
        out_shape=(out, out),
        in_specs=[any_spec, any_spec, any_spec, vmem, any_spec, any_spec, vmem],
        out_specs=(vmem, vmem),
        scratch_shapes=[
            pltpu.VMEM((devices, rows, wide), jnp.bfloat16),
            pltpu.VMEM((keys, 2 * depth), jnp.bfloat16),
            pltpu.VMEM((keys, 2 * depth), jnp.bfloat16),
            pltpu.VMEM((devices, 8, 128), jnp.int32),
            pltpu.VMEM(out_weight.shape, jnp.bfloat16),
            pltpu.VMEM((rows, width), jnp.bfloat16),
            pltpu.VMEM((2 * rows, wide), jnp.bfloat16),
            pltpu.VMEM((4, rows, width), jnp.float32),
            pltpu.VMEM((4, rows, width), jnp.bfloat16),
            pltpu.VMEM((4, rows, width), jnp.bfloat16),
            pltpu.VMEM((3, rows, width), jnp.bfloat16),
            pltpu.VMEM((2, rows, width // 2), jnp.bfloat16),
            pltpu.VMEM((2, rows, width), jnp.bfloat16),
            dma((devices,)), dma((devices,)), dma((devices,)), dma((devices,)),
            dma((devices,)), dma((devices,)), dma((devices,)), dma((devices,)),
            dma((2,)), dma((2,)), dma((8,)), dma((4,)), dma((4,)), dma((4,)), dma((4,)),
        ],
        compiler_params=pltpu.CompilerParams(
            collective_id=0, has_side_effects=True, vmem_limit_bytes=56 * 1024 * 1024
        ),
    )(
        queries,
        fresh_key_values,
        cache[0, 0],
        jnp.broadcast_to(lengths, (8, 128)),
        out_weight,
        residual,
        norm_gain[None, :],
    )


def per_device(
    queries,
    fresh_key_values,
    cache,
    lengths,
    out_weight,
    residual,
    norm_gain,
    expert_ids,
    gate_values,
    up_gate_weight,
    down_weight,
):
    seq_devices = lax.axis_size("sp")
    slot_rows = queries.shape[0]
    model_width = residual.shape[1]
    attended, normed = attention(
        queries, fresh_key_values, cache, lengths, out_weight, residual, norm_gain
    )
    own_live = jnp.arange(slot_rows, dtype=jnp.int32) < lengths[0, 0]
    group_count = lax.axis_size("grp")
    experts = up_gate_weight.shape[0] * group_count * seq_devices
    top_count = expert_ids.shape[1]
    capacity = max(2, 8 * slot_rows * top_count // (5 * experts))
    hidden_width = down_weight.shape[1]
    choose = expert_ids[:, :, None] == jnp.arange(experts, dtype=jnp.int32)[None, None, :]
    routed = (jnp.any(choose, axis=1) & own_live[:, None]).astype(jnp.float32)
    earlier = (jnp.arange(slot_rows)[:, None] > jnp.arange(slot_rows)[None, :]).astype(jnp.float32)
    prefix = jnp.dot(earlier, routed, precision=lax.Precision.HIGHEST)
    slot_in = jnp.sum(jnp.where(choose, prefix[:, None, :], 0.0), axis=2).astype(jnp.int32)
    dump_slot = experts * capacity
    target = jnp.where(own_live[:, None], expert_ids * capacity + slot_in, dump_slot)
    slot_range = jnp.arange(dump_slot, dtype=jnp.int32)
    hits = target.T[:, None, :] == slot_range[None, :, None]
    select = jnp.any(hits, axis=0).astype(jnp.bfloat16)
    outgoing = jnp.dot(select, normed, preferred_element_type=jnp.float32).astype(jnp.bfloat16)
    sectioned = outgoing.reshape(group_count, seq_devices, capacity, model_width)
    arrived = exchange_both(sectioned, ("grp", "sp"), ("grp", "sp"), (0, 1), (0, 1))
    flat_rows = arrived.reshape(-1, model_width)
    projected = jnp.dot(flat_rows, up_gate_weight[0], preferred_element_type=jnp.float32)
    hidden = (jax.nn.silu(projected[:, :hidden_width]) * projected[:, hidden_width:]).astype(
        jnp.bfloat16
    )
    returned = exchange_both(
        jnp.dot(hidden, down_weight[0], preferred_element_type=jnp.float32)
        .astype(jnp.bfloat16)
        .reshape(arrived.shape),
        ("grp", "sp"),
        ("grp", "sp"),
        (0, 1),
        (0, 1),
    )
    matches = target[:, :, None] == slot_range[None, None, :]
    mixing = jnp.sum(jnp.where(matches, gate_values[:, :, None], 0.0), axis=1)
    combined = jnp.dot(
        mixing.astype(jnp.bfloat16),
        returned.reshape(dump_slot, model_width),
        preferred_element_type=jnp.float32,
    )
    moe_out = jnp.where(own_live[:, None], combined, 0.0).astype(jnp.bfloat16)
    return (attended, moe_out)


def solution(mesh):
    in_specs = (
        P(("grp", "sp"), None),
        P(("grp", "sp"), None),
        P("grp", "sp", None, None),
        P("grp", "sp"),
        P("sp", None),
        P(("grp", "sp"), None),
        P(),
        P(("grp", "sp"), None),
        P(("grp", "sp"), None),
        P(("grp", "sp"), None, None),
        P(("grp", "sp"), None, None),
    )
    out_specs = (P(("grp", "sp"), None), P(("grp", "sp"), None))
    return jax.shard_map(
        per_device, mesh=mesh, in_specs=in_specs, out_specs=out_specs, check_vma=False
    )
```

time: 429 us -> 335 us (0.78)
  Pallas kernels: 0 us -> 64.3 us
  waiting for transfers between devices: 160 us -> 102 us
  matrix products: 69 us -> 39.8 us
  local copies, waits for them, and re-layouts: 25.7 us -> 2.66 us
  starting transfers between devices: 26 us -> 8.06 us
  other arithmetic: 24.2 us -> 7.63 us
  between operations: 14.9 us -> 1.54 us
    pallas_call x0 -> x1, Pallas kernels: none -> 64.3 us  [attention(): pl.pallas_call(group_attention, out_shape=(out, out), in_specs=[any_spec,...]
    reduce_scatter x1 -> x0, waiting for transfers between devices: 35.2 us -> none  [per_device(): lax.psum_scatter(jnp.dot(attn_heads, out_weight, preferred_element_type=j...]
    dot_general x5 -> x0, matrix products: 29.3 us -> none  [the longest x2 12.6 us: attend(): jnp.einsum('hrk,kd->hrd', weights.astype(jnp.bfloat16), value_all, prefer...]
    all_to_all x3 -> x0, waiting for transfers between devices: 22.9 us -> none  [the longest x1 12.6 us: per_device(): lax.all_to_all(queries, 'sp', split_axis=1, concat_axis=0, tiled=True)]
    all_to_all x3 -> x0, starting transfers between devices: 14.8 us -> none  [the longest x1 5.11 us: per_device(): lax.all_to_all(queries, 'sp', split_axis=1, concat_axis=0, tiled=True)]
    reduce_sum x4 -> x0, other arithmetic: 12.4 us -> none  [the longest x2 9.78 us: attend(): totals = jnp.sum(weights, axis=-1, keepdims=True)]
    dynamic_update_slice x4 -> x0, local copies, waits for them, and re-layouts: 8.29 us -> none  [per_device(): lax.map(attend, (queries_by_head.reshape(block_count, block_rows, per_dev...]
    reshape x5 -> x0, local copies, waits for them, and re-layouts: 5.96 us -> none  [the longest x1 3.58 us: per_device(): queries_by_head.reshape(block_count, block_rows, per_dev, head_width)]
  transfers between devices with their start and end apart: 6 -> 1, of which waited for: 4 -> 1; matrix products, arithmetic and copies ran while one was open for 5% -> 1% of each run, Pallas kernels for 0% -> 0%
where the time goes in v1:
time: 335 us; the launch traced here: 334 us
  blocking collectives  109 us (33%)
  waiting for transfers between devices  102 us (30%)
  Pallas kernels  64.3 us (19%)
  matrix products  39.8 us (12%)
  starting transfers between devices  8.06 us (2%)
  other arithmetic  7.63 us (2%)
    all_to_all x1, blocking collectives, exchange_both(): lax.all_to_all(pieces, axis, split_axis=0, concat_axis=0, tiled=True)  109 us
    all_to_all x1, waiting for transfers between devices, exchange_both(): lax.all_to_all(pieces, axis, split_axis=0, concat_axis=0, tiled=True)  102 us
    pallas_call x1, Pallas kernels, attention(): pl.pallas_call(group_attention, out_shape=(out, out), in_specs=[any_spec,...  64.3 us
    dot_general x1, matrix products, per_device(): jnp.dot(flat_rows, up_gate_weight[0], preferred_element_type=jnp.float32)  16 us
    dot_general x1, matrix products, per_device(): jnp.dot(hidden, down_weight[0], preferred_element_type=jnp.float32)  13.9 us
    all_to_all x1, starting transfers between devices, exchange_both(): lax.all_to_all(pieces, axis, split_axis=0, concat_axis=0, tiled=True)  8.06 us
  transfers between devices with their start and end apart: 1, of which 1 were waited for; matrix products, arithmetic and copies ran while one was open for 1% of the time, Pallas kernels for 0%

profile of v1, /device:TPU:1, one launch (start us, length us, event | category | flops | bytes accessed | tf_op | source)
XLA Modules:
  0.0 334.4 jit_solution(8057760332135467925)
XLA Ops:
  0.6 0.0 copy-start
  1.4 0.9 copy.28
  2.4 0.3 fusion.9
  2.7 0.2 fusion.10
  2.9 0.4 select_reduce_fusion.1
  3.4 0.1 copy.29
  3.5 0.7 add_select_fusion
  4.2 1.8 fusion
  6.0 0.6 broadcast_in_dim.72.lens_ref
  6.6 64.3 %shard_map.122 = (bf16[160,2048]{1,0:T(8,128)(2,1)}, bf16[160,2048]{1,0:T(8,128)(2,1)}) custom-call(bf16[160,4096]{1,0:T(8,128)(2,1)} %q_hbm.1, bf16[160,1024]{1,0:T(8,128)(2,1)} %fkv_hbm.1, bf16[256,256]{1,0:T(8,128)(2,1)} %bitcast.44, s32[8,128]{1,0:T(8,128)} %broadcast_in_dim.72.lens_ref, bf16[512,2048]{1,0:T(8,128)(2,1)} %w_hbm.1, ...), custom_call_target="tpu_custom_call" | custom-call | tf_op jit(solution)/shard_map/pallas_call | solution.py:321
  70.9 0.0 slice-start
  70.9 3.7 %convolution_convert_fusion.1 = bf16[2048,2048]{1,0:T(8,128)(2,1)S(1)} fusion(pred[2048,160]{0,1:T(8,128)(4,1)S(1)} %fusion, bf16[160,2048]{1,0:T(8,128)(2,1)} %get-tuple-element.5), kind=kOutput, calls=%fused_computation.5 | convolution fusion | flops 1346371584 | bytes 9371648 | tf_op jit(solution)/shard_map/dot_general | solution.py:393
  74.6 0.0 slice-start.1
  74.6 108.7 %all_to_all.10 = bf16[128,1,1,16,2048]{4,3,2,1,0:T(8,128)(2,1)S(1)} all-to-all(bf16[128,1,1,16,2048]{4,3,2,1,0:T(8,128)(2,1)S(1)} %bitcast.41), channel_id=1, replica_groups=mesh['grp'=16,'sp'=8] {'grp','sp'}, dimensions={0} | all-to-all | bytes 16777216 | tf_op jit(solution)/shard_map/all_to_all | solution.py:29
  183.4 0.0 slice-done
  183.4 16.0 %fusion.2 = f32[2048,1536]{1,0:T(8,128)} fusion(bf16[2048,2048]{1,0:T(8,128)(2,1)S(1)} %bitcast.43, bf16[1,2048,1536]{2,1,0:T(8,128)(2,1)S(1)} %bitcast.48), kind=kOutput, calls=%fused_computation.8 | convolution fusion | flops 12884901888 | bytes 27262976 | tf_op jit(solution)/shard_map/dot_general | solution.py:397
  199.4 13.9 %convolution_convert_fusion = bf16[2048,2048]{1,0:T(8,128)(2,1)} fusion(f32[2048,1536]{1,0:T(8,128)} %fusion.2, bf16[1,768,2048]{2,1,0:T(8,128)(2,1)S(1)} %copy-done), kind=kOutput, calls=%fused_computation.4 | convolution fusion | flops 6456082432 | bytes 24117248 | tf_op jit(solution)/shard_map/dot_general | solution.py:402
  213.3 8.1 %all-to-all-start.1 = ((bf16[128,1,1,16,2048]{4,3,2,1,0:T(8,128)(2,1)}), bf16[128,1,1,16,2048]{4,3,2,1,0:T(8,128)(2,1)}, u32[]{:S(2)}, u32[]{:S(2)}) async-start(bf16[128,1,1,16,2048]{4,3,2,1,0:T(8,128)(2,1)} %bitcast.42), calls=%async_computation.1 | async-start | bytes 16777216 | tf_op jit(solution)/shard_map/all_to_all | solution.py:29
  221.3 0.1 copy.30
  221.4 0.1 copy.31
  221.5 4.3 %select_reduce_fusion = bf16[160,2048]{1,0:T(8,128)(2,1)} fusion(f32[160,8]{1,0:T(8,128)S(1)} %copy.31, s32[160,8]{1,0:T(8,128)S(1)} %copy.30), kind=kLoop, calls=%fused_computation.1 | loop fusion | flops 7536640 | bytes 665600 | tf_op jit(solution)/shard_map/reduce_sum | solution.py:411
  225.9 101.6 %all-to-all-done.1 = bf16[128,1,1,16,2048]{4,3,2,1,0:T(8,128)(2,1)} async-done(((bf16[128,1,1,16,2048]{4,3,2,1,0:T(8,128)(2,1)}), bf16[128,1,1,16,2048]{4,3,2,1,0:T(8,128)(2,1)}, u32[]{:S(2)}, u32[]{:S(2)}) %all-to-all-start.1) | async-done | bytes 8388640 | tf_op jit(solution)/shard_map/all_to_all | solution.py:29
  327.5 6.0 %fusion.7 = bf16[160,2048]{1,0:T(8,128)(2,1)} fusion(bf16[2048,2048]{1,0:T(8,128)(2,1)} %bitcast.19, bf16[160,2048]{1,0:T(8,128)(2,1)} %select_reduce_fusion, pred[160]{0:T(512)(128)(4,1)S(1)} %iota_compare_fusion.5), kind=kOutput, calls=%fused_computation.13 | convolution fusion | flops 1342832640 | bytes 9699488 | tf_op jit(solution)/shard_map/dot_general | solution.py:412
  333.5 0.8 copy.36
  (8 shorter events, 0.0 us)
Async XLA Ops:
  0.6 198.7 %copy-start = (bf16[1,768,2048]{2,1,0:T(8,128)(2,1)S(1)}, bf16[1,768,2048]{2,1,0:T(8,128)(2,1)}, u32[]{:S(2)}) copy-start(bf16[1,768,2048]{2,1,0:T(8,128)(2,1)} %param.21) | copy-start | bytes 9437188
  70.9 112.4 %slice-start = ((s8[6291456]{0:T(1024)(128)(4,1)}), s8[2097152]{0:T(1024)(128)(4,1)S(1)}, s32[]{:S(2)}) async-start(s8[6291456]{0:T(1024)(128)(4,1)} %bitcast.47), calls=%async_computation.2 | async-start | bytes 4194304
  74.6 108.7 %slice-start.1 = ((s8[6291456]{0:T(1024)(128)(4,1)}), s8[4194304]{0:T(1024)(128)(4,1)S(1)}, s32[]{:S(2)}) async-start(s8[6291456]{0:T(1024)(128)(4,1)} %bitcast.47), calls=%async_computation.3 | async-start | bytes 8388608
  213.3 8.2 %copy-start.2 = (f32[160,8]{0,1:T(8,128)S(1)}, f32[160,8]{0,1:T(8,128)}, u32[]{:S(2)}) copy-start(f32[160,8]{0,1:T(8,128)} %param.19) | copy-start | bytes 15364
  213.3 114.2 %all-to-all-start.1 = ((bf16[128,1,1,16,2048]{4,3,2,1,0:T(8,128)(2,1)}), bf16[128,1,1,16,2048]{4,3,2,1,0:T(8,128)(2,1)}, u32[]{:S(2)}, u32[]{:S(2)}) async-start(bf16[128,1,1,16,2048]{4,3,2,1,0:T(8,128)(2,1)} %bitcast.42), calls=%async_computation.1 | async-start | bytes 16777216 | tf_op jit(solution)/shard_map/all_to_all | solution.py:29
  327.5 6.0 %copy-start.1 = (bf16[160,2048]{1,0:T(8,128)(2,1)S(1)}, bf16[160,2048]{1,0:T(8,128)(2,1)}, u32[]{:S(2)}) copy-start(bf16[160,2048]{1,0:T(8,128)(2,1)} %get-tuple-element.8) | copy-start | bytes 1966084

commit v2 on v1

--- a/solution.py
+++ b/solution.py
@@ -7,28 +7,6 @@
 from jax.experimental import pallas as pl
 from jax.experimental.pallas import tpu as pltpu
 from jax.sharding import PartitionSpec as P
-
-
-def in_order(pieces, dim):
-    shape = list(pieces.shape[1:])
-    shape[dim] *= pieces.shape[0]
-    return jnp.moveaxis(pieces, 0, dim).reshape(shape)
-
-
-def split_up(x, dim, devices):
-    before, after = (x.shape[:dim], x.shape[dim + 1 :])
-    return jnp.moveaxis(x.reshape(*before, devices, -1, *after), dim, 0)
-
-
-def exchange_both(x, axis, axes, splits, concats):
-    sizes = [lax.axis_size(a) for a in axes]
-    pieces = split_up(x, splits[0], sizes[0])
-    pieces = jnp.moveaxis(split_up(pieces, splits[1] + 1, sizes[1]), 0, 1)
-    inside = pieces.shape[2:]
-    pieces = pieces.reshape(-1, *inside)
-    pieces = lax.all_to_all(pieces, axis, split_axis=0, concat_axis=0, tiled=True)
-    pieces = in_order(pieces.reshape(*sizes, *inside), concats[0] + 1)
-    return in_order(pieces, concats[1])
 
 
 MESH = pl.DeviceIdType.MESH
@@ -355,6 +333,315 @@
     )
 
 
+SLOTS = 16
+
+
+def expert_exchange(
+    line, columns,
+    normed_hbm, meta_hbm, up_hbm, down_hbm,
+    out_ref,
+    xg0, xg1, xg2, meta, sb0, sb1, sb2, recv, ready, rt0, rt1, rt2,
+    rs0, rs1, rs2, pb0, pb1, pb2, up, down, hidden,
+    w_sem, meta_send, meta_recv, x_send, x_recv, d_send, d_recv,
+    r_send, r_recv, s_send, s_recv,
+):
+    xg, sb, rt, rs, pb = (xg0, xg1, xg2), (sb0, sb1, sb2), (rt0, rt1, rt2), (rs0, rs1, rs2), (pb0, pb1, pb2)
+    grp, sp = lax.axis_index("grp"), lax.axis_index("sp")
+    pos = (grp // line, sp // 2, lax.rem(grp, line))
+    core = lax.rem(sp, 2)
+    rows = meta.shape[3]
+    plane = 2 * line * line
+    ff, width = down.shape
+
+    def wrap(value):
+        return lax.rem(value + 2 * line, line)
+
+    def device(p, cc):
+        return (p[0] * line + p[2], p[1] * 2 + cc)
+
+    def others(a):
+        return (a + 1) % 3, (a + 2) % 3
+
+    def moved(p, a, value):
+        p = list(p)
+        p[a] = value
+        return p
+
+    def source(group, a, p):
+        i, j = others(a)
+        return wrap(group - p[i] - p[j])
+
+    def cols(a):
+        return pl.ds(columns[a][0], columns[a][1])
+
+    bar = pltpu.get_barrier_semaphore()
+    peers = [
+        (dx, dy, dz, dc)
+        for dx in range(line) for dy in range(line) for dz in range(line) for dc in range(2)
+        if dx * dy * dz == 0 and (dx, dy, dz, dc) != (0, 0, 0, 0)
+    ]
+    for dx, dy, dz, dc in peers:
+        p = (lax.rem(pos[0] + dx, line), lax.rem(pos[1] + dy, line), lax.rem(pos[2] + dz, line))
+        pl.semaphore_signal(
+            bar, inc=1, device_id=device(p, lax.rem(core + dc, 2)), device_id_type=MESH
+        )
+    weights = (
+        pltpu.make_async_copy(up_hbm.at[0], up, w_sem.at[0]),
+        pltpu.make_async_copy(down_hbm.at[0], down, w_sem.at[1]),
+    )
+    for copy in weights:
+        copy.start()
+    for a in range(3):
+        pltpu.make_async_copy(meta_hbm, meta.at[a, pos[a]], meta_recv.at[a, pos[a]]).start()
+        pltpu.make_async_copy(
+            normed_hbm.at[:, cols(a)], xg[a].at[pos[a]], x_recv.at[a, pos[a]]
+        ).start()
+    pl.semaphore_wait(bar, len(peers))
+
+    def meta_copy(a, k):
+        to = device(moved(pos, a, lax.rem(pos[a] + k, line)), core)
+        return pltpu.make_async_remote_copy(
+            meta_hbm, meta.at[a, pos[a]], meta_send.at[a, k], meta_recv.at[a, pos[a]],
+            device_id=to, device_id_type=MESH,
+        )
+
+    def x_copy(a, k):
+        to = device(moved(pos, a, lax.rem(pos[a] + k, line)), core)
+        return pltpu.make_async_remote_copy(
+            normed_hbm.at[:, cols(a)], xg[a].at[pos[a]], x_send.at[a, k], x_recv.at[a, pos[a]],
+            device_id=to, device_id_type=MESH,
+        )
+
+    hops = sorted(range(1, line), key=lambda k: (min(k, line - k), k))
+    for k in hops:
+        for a in range(3):
+            meta_copy(a, k).start()
+    for k in hops:
+        for a in range(3):
+            x_copy(a, k).start()
+    for a in range(3):
+        for i in range(line):
+            pltpu.make_async_copy(meta.at[a, i], meta.at[a, i], meta_recv.at[a, i]).wait()
+
+    shift = line.bit_length() - 1
+    q = lax.broadcasted_iota(jnp.int32, (plane, rows), 0)
+    q_u = lax.shift_right_logical(q, shift + 1)
+    q_v = lax.bitwise_and(lax.shift_right_logical(q, 1), line - 1)
+    q_c = lax.bitwise_and(q, 1)
+    big = (plane * SLOTS, plane)
+    spread = jnp.where(
+        lax.shift_right_logical(lax.broadcasted_iota(jnp.int32, big, 0), 4)
+        == lax.broadcasted_iota(jnp.int32, big, 1),
+        1.0,
+        0.0,
+    ).astype(jnp.bfloat16)
+    slot = (
+        lax.bitwise_and(lax.broadcasted_iota(jnp.int32, (plane * SLOTS, rows), 0), SLOTS - 1) + 1
+    ).astype(jnp.float32)
+
+    def routing(a, i, gated):
+        u, v = others(a)
+        where = [None, None, None]
+        where[a], where[u], where[v] = pos[a], q_u, q_v
+        expert = ((where[0] * line + where[2]) * line + where[1]) * 2 + q_c
+        expert = expert.astype(jnp.float32)
+        info = meta[a, i]
+        place = jnp.zeros((plane, rows), jnp.float32)
+        gate = jnp.zeros((plane, rows), jnp.float32)
+        for k in range(8):
+            match = info[k : k + 1, :] == expert
+            place = place + jnp.where(match, info[8 + k : 9 + k, :], 0.0)
+            if gated:
+                gate = gate + jnp.where(match, info[16 + k : 17 + k, :], 0.0)
+        hit = jnp.dot(spread, place.astype(jnp.bfloat16), preferred_element_type=jnp.float32) == slot
+        if gated:
+            value = jnp.dot(spread, gate.astype(jnp.bfloat16), preferred_element_type=jnp.float32)
+        else:
+            value = 1.0
+        return jnp.where(hit, value, 0.0).astype(jnp.bfloat16)
+
+    steps = [(0, 0)] + sorted(
+        [(i, j) for i in range(line) for j in range(line) if (i, j) != (0, 0)],
+        key=lambda o: (
+            min(o[0], line - o[0]) + min(o[1], line - o[1]),
+            sorted((min(o[0], line - o[0]), min(o[1], line - o[1]))),
+        ),
+    )
+
+    def plane_peer(a, step, dc):
+        u, v = others(a)
+        p = moved(pos, u, lax.rem(pos[u] + step[0], line))
+        p = moved(p, v, lax.rem(pos[v] + step[1], line))
+        return p, lax.rem(core + dc, 2)
+
+    def index_in_plane(a, p, cc):
+        u, v = others(a)
+        return (p[u] * line + p[v]) * 2 + cc
+
+    def spots():
+        for step in steps:
+            for dc in range(2):
+                for a in range(3):
+                    yield a, step, dc
+
+    def dispatch(group, carry):
+        for a in range(3):
+            i = source(group, a, pos)
+            pltpu.make_async_copy(xg[a].at[i], xg[a].at[i], x_recv.at[a, i]).wait()
+            picked = jnp.dot(
+                routing(a, i, False), xg[a][i], preferred_element_type=jnp.float32
+            ).astype(jnp.bfloat16)
+            sb[a][group] = picked.reshape(plane, SLOTS, columns[a][1])
+        for a, step, dc in spots():
+            p, cc = plane_peer(a, step, dc)
+            d = moved(pos, a, source(group, a, pos))
+            src = sb[a].at[group, index_in_plane(a, p, cc)]
+            dst = recv.at[group, d[0], d[2], core, :, cols(a)]
+            if step == (0, 0) and dc == 0:
+                pltpu.make_async_copy(src, dst, d_recv.at[group]).start()
+            else:
+                pltpu.make_async_remote_copy(
+                    src, dst, d_send.at[a, group], d_recv.at[group],
+                    device_id=device(p, cc), device_id_type=MESH,
+                ).start()
+        return carry
+
+    lax.fori_loop(0, line, dispatch, 0)
+    for copy in weights:
+        copy.wait()
+
+    block = min(256, ff)
+    wide = min(512, width)
+
+    def experts(group, carry):
+        pltpu.make_async_copy(recv.at[group], recv.at[group], d_recv.at[group]).wait()
+
+        def first(j, inner):
+            x = recv[group].reshape(plane * SLOTS, width)
+            at = pl.multiple_of(j * block, block)
+            gate = jnp.dot(x, up[:, pl.ds(at, block)], preferred_element_type=jnp.float32)
+            lift = jnp.dot(x, up[:, pl.ds(ff + at, block)], preferred_element_type=jnp.float32)
+            hidden[:, pl.ds(at, block)] = (gate / (1.0 + jnp.exp(-gate)) * lift).astype(jnp.bfloat16)
+            return inner
+
+        lax.fori_loop(0, ff // block, first, 0)
+
+        def second(j, inner):
+            at = pl.multiple_of(j * wide, wide)
+            value = jnp.dot(
+                hidden[...], down[:, pl.ds(at, wide)], preferred_element_type=jnp.float32
+            )
+            ready[group, :, :, :, :, pl.ds(at, wide)] = value.astype(jnp.bfloat16).reshape(
+                line, line, 2, SLOTS, wide
+            )
+            return inner
+
+        lax.fori_loop(0, width // wide, second, 0)
+        for a, step, dc in spots():
+            p, cc = plane_peer(a, step, dc)
+            d = moved(p, a, source(group, a, p))
+            src = ready.at[group, d[0], d[2], cc, :, cols(a)]
+            dst = rt[a].at[group, index_in_plane(a, pos, core)]
+            if step == (0, 0) and dc == 0:
+                pltpu.make_async_copy(src, dst, r_recv.at[a, group]).start()
+            else:
+                pltpu.make_async_remote_copy(
+                    src, dst, r_send.at[a, group], r_recv.at[a, group],
+                    device_id=device(p, cc), device_id_type=MESH,
+                ).start()
+        return carry
+
+    lax.fori_loop(0, line, experts, 0)
+
+    def s_copy(a, i):
+        to = device(moved(pos, a, i), core)
+        return pltpu.make_async_remote_copy(
+            pb[a].at[i], rs[a].at[pos[a]], s_send.at[a, i], s_recv.at[a, pos[a]],
+            device_id=to, device_id_type=MESH,
+        )
+
+    def combine(group, carry):
+        for a in range(3):
+            i = source(group, a, pos)
+            pltpu.make_async_copy(rt[a].at[group], rt[a].at[group], r_recv.at[a, group]).wait()
+            share = lax.dot_general(
+                routing(a, i, True),
+                rt[a][group].reshape(plane * SLOTS, columns[a][1]),
+                (((0,), (0,)), ((), ())),
+                preferred_element_type=jnp.float32,
+            )
+            pb[a][i] = share.astype(jnp.bfloat16)
+
+            @pl.when(i != pos[a])
+            def _():
+                s_copy(a, i).start()
+
+        return carry
+
+    lax.fori_loop(0, line, combine, 0)
+    for a in range(3):
+        total = pb[a][pos[a]].astype(jnp.float32)
+        for k in range(1, line):
+            i = lax.rem(pos[a] + k, line)
+            pltpu.make_async_copy(rs[a].at[i], rs[a].at[i], s_recv.at[a, i]).wait()
+            total = total + rs[a][i].astype(jnp.float32)
+        out_ref[:, columns[a][0] : columns[a][0] + columns[a][1]] = total.astype(jnp.bfloat16)
+
+    for a in range(3):
+        for k in range(1, line):
+            meta_copy(a, k).wait_send()
+            x_copy(a, k).wait_send()
+            s_copy(a, lax.rem(pos[a] + k, line)).wait_send()
+        for group in range(line):
+            sent = sb[a].at[group, pl.ds(0, plane - 1)]
+            pltpu.make_async_copy(sent, sent, d_send.at[a, group]).wait()
+            back = rt[a].at[group, pl.ds(0, plane - 1)]
+            pltpu.make_async_copy(back, back, r_send.at[a, group]).wait()
+
+
+def mix_experts(normed, meta, up_gate_weight, down_weight):
+    line = math.isqrt(lax.axis_size("grp"))
+    rows, width = normed.shape
+    ff = down_weight.shape[1]
+    plane = 2 * line * line
+    tiles = width // 128
+    cuts = [0, tiles // 3, 2 * (tiles // 3), tiles]
+    columns = [(128 * cuts[a], 128 * (cuts[a + 1] - cuts[a])) for a in range(3)]
+    any_spec = pl.BlockSpec(memory_space=pl.ANY)
+    dma = pltpu.SemaphoreType.DMA
+
+    def buffers(*shape):
+        return [pltpu.VMEM((*shape, columns[a][1]), jnp.bfloat16) for a in range(3)]
+
+    whole = pltpu.VMEM((line, line, line, 2, SLOTS, width), jnp.bfloat16)
+    return pl.pallas_call(
+        functools.partial(expert_exchange, line, columns),
+        out_shape=jax.ShapeDtypeStruct((rows, width), jnp.bfloat16),
+        in_specs=[any_spec] * 4,
+        out_specs=pl.BlockSpec(memory_space=pltpu.VMEM),
+        scratch_shapes=[
+            *buffers(line, rows),
+            pltpu.VMEM((3, line, *meta.shape), jnp.float32),
+            *buffers(line, plane, SLOTS),
+            whole,
+            whole,
+            *buffers(line, plane, SLOTS),
+            *buffers(line, rows),
+            *buffers(line, rows),
+            pltpu.VMEM(up_gate_weight.shape[1:], jnp.bfloat16),
+            pltpu.VMEM(down_weight.shape[1:], jnp.bfloat16),
+            pltpu.VMEM((plane * SLOTS, ff), jnp.bfloat16),
+            dma((2,)),
+            dma((3, line)), dma((3, line)), dma((3, line)), dma((3, line)),
+            dma((3, line)), dma((line,)), dma((3, line)), dma((3, line)),
+            dma((3, line)), dma((3, line)),
+        ],
+        compiler_params=pltpu.CompilerParams(
+            collective_id=1, has_side_effects=True, vmem_limit_bytes=67_000_000
+        ),
+    )(normed, meta, up_gate_weight, down_weight)
+
+
 def per_device(
     queries,
     fresh_key_values,
@@ -370,52 +657,19 @@
 ):
     seq_devices = lax.axis_size("sp")
     slot_rows = queries.shape[0]
-    model_width = residual.shape[1]
     attended, normed = attention(
         queries, fresh_key_values, cache, lengths, out_weight, residual, norm_gain
     )
     own_live = jnp.arange(slot_rows, dtype=jnp.int32) < lengths[0, 0]
-    group_count = lax.axis_size("grp")
-    experts = up_gate_weight.shape[0] * group_count * seq_devices
-    top_count = expert_ids.shape[1]
-    capacity = max(2, 8 * slot_rows * top_count // (5 * experts))
-    hidden_width = down_weight.shape[1]
+    experts = up_gate_weight.shape[0] * lax.axis_size("grp") * lax.axis_size("sp")
     choose = expert_ids[:, :, None] == jnp.arange(experts, dtype=jnp.int32)[None, None, :]
     routed = (jnp.any(choose, axis=1) & own_live[:, None]).astype(jnp.float32)
     earlier = (jnp.arange(slot_rows)[:, None] > jnp.arange(slot_rows)[None, :]).astype(jnp.float32)
     prefix = jnp.dot(earlier, routed, precision=lax.Precision.HIGHEST)
-    slot_in = jnp.sum(jnp.where(choose, prefix[:, None, :], 0.0), axis=2).astype(jnp.int32)
-    dump_slot = experts * capacity
-    target = jnp.where(own_live[:, None], expert_ids * capacity + slot_in, dump_slot)
-    slot_range = jnp.arange(dump_slot, dtype=jnp.int32)
-    hits = target.T[:, None, :] == slot_range[None, :, None]
-    select = jnp.any(hits, axis=0).astype(jnp.bfloat16)
-    outgoing = jnp.dot(select, normed, preferred_element_type=jnp.float32).astype(jnp.bfloat16)
-    sectioned = outgoing.reshape(group_count, seq_devices, capacity, model_width)
-    arrived = exchange_both(sectioned, ("grp", "sp"), ("grp", "sp"), (0, 1), (0, 1))
-    flat_rows = arrived.reshape(-1, model_width)
-    projected = jnp.dot(flat_rows, up_gate_weight[0], preferred_element_type=jnp.float32)
-    hidden = (jax.nn.silu(projected[:, :hidden_width]) * projected[:, hidden_width:]).astype(
-        jnp.bfloat16
-    )
-    returned = exchange_both(
-        jnp.dot(hidden, down_weight[0], preferred_element_type=jnp.float32)
-        .astype(jnp.bfloat16)
-        .reshape(arrived.shape),
-        ("grp", "sp"),
-        ("grp", "sp"),
-        (0, 1),
-        (0, 1),
-    )
-    matches = target[:, :, None] == slot_range[None, None, :]
-    mixing = jnp.sum(jnp.where(matches, gate_values[:, :, None], 0.0), axis=1)
-    combined = jnp.dot(
-        mixing.astype(jnp.bfloat16),
-        returned.reshape(dump_slot, model_width),
-        preferred_element_type=jnp.float32,
-    )
-    moe_out = jnp.where(own_live[:, None], combined, 0.0).astype(jnp.bfloat16)
-    return (attended, moe_out)
+    slot_in = jnp.sum(jnp.where(choose, prefix[:, None, :], 0.0), axis=2)
+    chosen = jnp.where(own_live[:, None], expert_ids, experts).astype(jnp.float32)
+    meta = jnp.concatenate([chosen, slot_in + 1.0, gate_values], axis=1).T
+    return (attended, mix_experts(normed, meta, up_gate_weight, down_weight))
 
 
 def solution(mesh):

time: 335 us -> 240 us (0.72)
  Pallas kernels: 64.3 us -> 228 us
  blocking collectives: 109 us -> 0 us
  waiting for transfers between devices: 102 us -> 0 us
  matrix products: 39.8 us -> 0.22 us
  starting transfers between devices: 8.06 us -> 0 us
  other arithmetic: 7.63 us -> 2.79 us
    pallas_call x0 -> x1, Pallas kernels: none -> 164 us  [mix_experts(): pl.pallas_call(functools.partial(expert_exchange, line, columns), out_sha...]
    all_to_all x1 -> x0, blocking collectives: 109 us -> none  [exchange_both(): lax.all_to_all(pieces, axis, split_axis=0, concat_axis=0, tiled=True)]
    all_to_all x1 -> x0, waiting for transfers between devices: 102 us -> none  [exchange_both(): lax.all_to_all(pieces, axis, split_axis=0, concat_axis=0, tiled=True)]
    dot_general x4 -> x0, matrix products: 39.6 us -> none  [the longest x1 16 us: per_device(): jnp.dot(flat_rows, up_gate_weight[0], preferred_element_type=jnp.float32)]
    all_to_all x1 -> x0, starting transfers between devices: 8.06 us -> none  [exchange_both(): lax.all_to_all(pieces, axis, split_axis=0, concat_axis=0, tiled=True)]
    reduce_sum x2 -> x1, other arithmetic: 4.76 us -> 0.44 us  [per_device(): slot_in = jnp.sum(jnp.where(choose, prefix[:, None, :], 0.0), axis=2)]
  transfers between devices with their start and end apart: 1 -> 0, of which waited for: 1 -> 0; matrix products, arithmetic and copies ran while one was open for 1% -> 0% of each run, Pallas kernels for 0% -> 0%
where the time goes in v2:
time: 240 us; the launch traced here: 238 us
  Pallas kernels  228 us (95%)
  local copies, waits for them, and re-layouts  5.41 us (2%)
  other arithmetic  2.79 us (1%)
    pallas_call x1, Pallas kernels, mix_experts(): pl.pallas_call(functools.partial(expert_exchange, line, columns), out_sha...  164 us
    pallas_call x1, Pallas kernels, attention(): pl.pallas_call(group_attention, out_shape=(out, out), in_specs=[any_spec,...  64.3 us

profile of v2, /device:TPU:1, one launch (start us, length us, event | category | flops | bytes accessed | tf_op | source)
XLA Modules:
  0.0 237.6 jit_solution(12861035289037112859)
XLA Ops:
  1.3 0.6 broadcast_in_dim.42.lens_ref
  1.9 0.7 select_convert_fusion
  2.6 0.8 copy.14
  3.4 0.3 fusion
  3.7 0.2 fusion.1
  3.9 0.4 select_reduce_fusion
  4.4 0.1 copy.15
  4.4 1.3 maximum_bitcast_fusion.meta_hbm
  5.8 64.3 %shard_map.122 = (bf16[160,2048]{1,0:T(8,128)(2,1)}, bf16[160,2048]{1,0:T(8,128)(2,1)}) custom-call(bf16[160,4096]{1,0:T(8,128)(2,1)} %q_hbm.1, bf16[160,1024]{1,0:T(8,128)(2,1)} %fkv_hbm.1, bf16[256,256]{1,0:T(8,128)(2,1)} %bitcast.7, s32[8,128]{1,0:T(8,128)} %broadcast_in_dim.42.lens_ref, bf16[512,2048]{1,0:T(8,128)(2,1)} %w_hbm.1, ...), custom_call_target="tpu_custom_call" | custom-call | tf_op jit(solution)/shard_map/pallas_call | solution.py:299
  70.1 163.6 %shard_map.123 = bf16[160,2048]{1,0:T(8,128)(2,1)} custom-call(bf16[160,2048]{1,0:T(8,128)(2,1)} %get-tuple-element.5.normed_hbm, f32[24,160]{1,0:T(8,128)} %maximum_bitcast_fusion.meta_hbm, bf16[1,2048,1536]{2,1,0:T(8,128)(2,1)} %up_hbm.1, bf16[1,768,2048]{2,1,0:T(8,128)(2,1)} %down_hbm.1), custom_call_target="tpu_custom_call" | custom-call | tf_op jit(solution)/shard_map/pallas_call | solution.py:617
  233.7 2.0 copy.19
  235.7 2.0 copy.20
  (2 shorter events, 0.0 us)

commit v3 on v2

v3 whole, which is shorter than its diff:
```python
import functools
import math

import jax
import jax.numpy as jnp
from jax import lax
from jax.experimental import pallas as pl
from jax.experimental.pallas import tpu as pltpu
from jax.sharding import PartitionSpec as P

MESH = pl.DeviceIdType.MESH
NEG = -1e30
SLOTS = 16


def layer(
    line, columns,
    q_hbm, fkv_hbm, cache_hbm, lens_ref, w_hbm, res_hbm, gain_ref, ids_ref, gates_ref, up_hbm, down_hbm,
    attn_ref, moe_ref,
    qb, kx, vx, lb, w, res, heads, own, mine, parts, normed, info,
    xg, meta, sb, recv, rt, rs, pb, up, down, hidden,
    q_send, k_send, v_send, l_send, q_recv, k_recv, v_recv, l_recv,
    c_send, c_recv, local, pair_send, pair_recv, part_send, part_recv,
    w_sem, meta_send, meta_recv, x_send, x_recv, d_send, d_recv,
    r_send, r_recv, s_send, s_recv,
):
    grp, me = lax.axis_index("grp"), lax.axis_index("sp")
    pos = (grp // line, me // 2, lax.rem(grp, line))
    core = lax.rem(me, 2)
    devices, chips = 2 * line, line
    rows, wide = qb.shape[1], qb.shape[2]
    depth = kx.shape[1] // 2
    per = wide // depth
    block = cache_hbm.shape[0]
    cached = 2 * block
    y, c = pos[1], core
    partner = y * 2 + 1 - c
    plane = 2 * line * line
    ff, width = down.shape
    tiles = rows // SLOTS

    def wrap(value):
        return lax.rem(value + 2 * line, line)

    def device(p, cc):
        return (p[0] * line + p[2], p[1] * 2 + cc)

    def others(a):
        return (a + 1) % 3, (a + 2) % 3

    def moved(p, a, value):
        p = list(p)
        p[a] = value
        return p

    def source(group, a, p):
        i, j = others(a)
        return wrap(group - p[i] - p[j])

    def cols(a):
        return pl.ds(columns[a][0], columns[a][1])

    def span(a):
        return slice(columns[a][0], columns[a][0] + columns[a][1])

    bar = pltpu.get_barrier_semaphore()
    peers = [
        (dx, dy, dz, dc)
        for dx in range(line) for dy in range(line) for dz in range(line) for dc in range(2)
        if dx * dy * dz == 0 and (dx, dy, dz, dc) != (0, 0, 0, 0)
    ]
    for dx, dy, dz, dc in peers:
        p = (lax.rem(pos[0] + dx, line), lax.rem(pos[1] + dy, line), lax.rem(pos[2] + dz, line))
        pl.semaphore_signal(
            bar, inc=1, device_id=device(p, lax.rem(core + dc, 2)), device_id_type=MESH
        )

    pltpu.make_async_copy(q_hbm.at[:, pl.ds(me * wide, wide)], qb.at[me], q_recv.at[me]).start()
    local_copies = [
        pltpu.make_async_copy(w_hbm, w, local.at[0]),
        pltpu.make_async_copy(res_hbm, res, local.at[1]),
        pltpu.make_async_copy(
            cache_hbm.at[:, pl.ds(0, depth)],
            kx.at[pl.ds(c * block, block), pl.ds(0, depth)],
            local.at[2],
        ),
        pltpu.make_async_copy(
            cache_hbm.at[:, pl.ds(depth, depth)],
            vx.at[pl.ds(c * block, block), pl.ds(0, depth)],
            local.at[3],
        ),
        pltpu.make_async_copy(
            fkv_hbm.at[:, pl.ds(y * depth, depth)],
            kx.at[pl.ds(cached + me * rows, rows), pl.ds(0, depth)],
            local.at[4],
        ),
        pltpu.make_async_copy(
            fkv_hbm.at[:, pl.ds((chips + y) * depth, depth)],
            vx.at[pl.ds(cached + me * rows, rows), pl.ds(0, depth)],
            local.at[5],
        ),
        pltpu.make_async_copy(lens_ref, lb.at[me], local.at[6]),
    ]
    for copy in local_copies:
        copy.start()
    weights = (
        pltpu.make_async_copy(up_hbm.at[0], up, w_sem.at[0]),
        pltpu.make_async_copy(down_hbm.at[0], down, w_sem.at[1]),
    )
    vx[:, depth:] = jnp.ones((vx.shape[0], depth), jnp.bfloat16)
    kx[:cached, depth:] = jnp.zeros((cached, depth), jnp.bfloat16)

    pl.semaphore_wait(bar, len(peers))

    def k_copy(i):
        p = lax.rem(me + i, devices)
        return pltpu.make_async_remote_copy(
            fkv_hbm.at[:, pl.ds((p // 2) * depth, depth)],
            kx.at[pl.ds(cached + me * rows, rows), pl.ds(0, depth)],
            k_send.at[i], k_recv.at[me], device_id={"sp": p}, device_id_type=MESH,
        )

    def v_copy(i):
        p = lax.rem(me + i, devices)
        return pltpu.make_async_remote_copy(
            fkv_hbm.at[:, pl.ds((chips + p // 2) * depth, depth)],
            vx.at[pl.ds(cached + me * rows, rows), pl.ds(0, depth)],
            v_send.at[i], v_recv.at[me], device_id={"sp": p}, device_id_type=MESH,
        )

    def l_copy(i):
        p = lax.rem(me + i, devices)
        return pltpu.make_async_remote_copy(
            lens_ref, lb.at[me], l_send.at[i], l_recv.at[me],
            device_id={"sp": p}, device_id_type=MESH,
        )

    def q_copy(i):
        p = lax.rem(me + i, devices)
        return pltpu.make_async_remote_copy(
            q_hbm.at[:, pl.ds(p * wide, wide)], qb.at[me], q_send.at[i], q_recv.at[me],
            device_id={"sp": p}, device_id_type=MESH,
        )

    cache_copies = [
        pltpu.make_async_remote_copy(
            cache_hbm.at[:, pl.ds(d * depth, depth)],
            dst.at[pl.ds(c * block, block), pl.ds(0, depth)],
            c_send.at[d], c_recv.at[d], device_id={"sp": partner}, device_id_type=MESH,
        )
        for d, dst in enumerate((kx, vx))
    ]
    far_first = sorted(range(1, devices), key=lambda i: -min(i, devices - i))
    for i in far_first:
        k_copy(i).start()
        v_copy(i).start()
        l_copy(i).start()
    for copy in cache_copies:
        copy.start()
    for i in far_first:
        q_copy(i).start()
    for copy in weights:
        copy.start()

    experts = plane * line
    lanes = lax.broadcasted_iota(jnp.int32, (8, rows), 1)
    living = lanes < lens_ref[:, 0:1]
    expert_rows = lax.broadcasted_iota(jnp.int32, (experts, rows), 0)
    named = jnp.where(living, ids_ref[...], experts)
    routed = jnp.zeros((experts, rows), jnp.float32)
    for k in range(8):
        routed = routed + jnp.where(named[k : k + 1, :] == expert_rows, 1.0, 0.0)
    square = (rows, rows)
    before = jnp.where(
        lax.broadcasted_iota(jnp.int32, square, 0) < lax.broadcasted_iota(jnp.int32, square, 1),
        1.0,
        0.0,
    ).astype(jnp.bfloat16)
    prefix = jnp.dot(routed.astype(jnp.bfloat16), before, preferred_element_type=jnp.float32)
    info[0:8, :] = named.astype(jnp.float32)
    for k in range(8):
        hits = jnp.where(named[k : k + 1, :] == expert_rows, prefix, 0.0)
        info[8 + k : 9 + k, :] = jnp.sum(hits, axis=0, keepdims=True) + 1.0
    info[16:24, :] = gates_ref[...]

    for copy in local_copies:
        copy.wait()
    for copy in cache_copies:
        copy.wait_recv()
    row_ids = lax.broadcasted_iota(jnp.int32, (rows, depth), 0)
    for i in range(1, devices):
        t = lax.rem(me + i, devices)
        at = pl.ds(cached + t * rows, rows)
        left = pl.ds(0, depth)
        pltpu.make_async_copy(lb.at[t], lb.at[t], l_recv.at[t]).wait()
        pltpu.make_async_copy(kx.at[at, left], kx.at[at, left], k_recv.at[t]).wait()
        pltpu.make_async_copy(vx.at[at, left], vx.at[at, left], v_recv.at[t]).wait()
    for t in range(devices):
        alive = row_ids < lb[t, 0:1, :]
        kx[cached + t * rows : cached + (t + 1) * rows, depth:] = jnp.where(
            alive, 0.0, NEG
        ).astype(jnp.bfloat16)

    def meta_copy(a, k):
        to = device(moved(pos, a, lax.rem(pos[a] + k, line)), core)
        return pltpu.make_async_remote_copy(
            info, meta.at[a, pos[a]], meta_send.at[a, k], meta_recv.at[a, pos[a]],
            device_id=to, device_id_type=MESH,
        )

    for a in range(3):
        pltpu.make_async_copy(info, meta.at[a, pos[a]], meta_recv.at[a, pos[a]]).start()
        for k in range(1, line):
            meta_copy(a, k).start()

    scale = math.log2(math.e) / math.sqrt(depth)
    pair_rows = 2 * rows
    lane = lax.broadcasted_iota(jnp.int32, (pair_rows, depth), 1)
    pick = jnp.where(lane == 0, 1.0, 0.0).astype(jnp.bfloat16)

    def attend(chip):
        keys = cached + (chip + 1) * pair_rows
        first = (cached + chip * pair_rows) // 128 * 128
        shift = cached + chip * pair_rows - first

        def head(h, carry):
            q = qb[2 * chip : 2 * chip + 2, :, pl.ds(pl.multiple_of(h * depth, depth), depth)]
            q = jnp.concatenate([q.reshape(pair_rows, depth), pick], axis=1)
            dims = (((1,), (1,)), ((), ()))
            sa = lax.dot_general(q, kx[:first, :], dims, preferred_element_type=jnp.float32)
            sb = lax.dot_general(q, kx[first:keys, :], dims, preferred_element_type=jnp.float32)
            i = lax.broadcasted_iota(jnp.int32, sb.shape, 0)
            j = lax.broadcasted_iota(jnp.int32, sb.shape, 1)
            sb = jnp.where(j - shift <= i, sb, NEG)
            top = jnp.maximum(
                jnp.max(sa, axis=1, keepdims=True), jnp.max(sb, axis=1, keepdims=True)
            )
            pa = jnp.exp2((sa - top) * scale).astype(jnp.bfloat16)
            pb = jnp.exp2((sb - top) * scale).astype(jnp.bfloat16)
            out = jnp.dot(pa, vx[:first, :], preferred_element_type=jnp.float32)
            out = out + jnp.dot(pb, vx[first:keys, :], preferred_element_type=jnp.float32)
            heads[:, pl.ds(pl.multiple_of(h * depth, depth), depth)] = (
                out[:, :depth] / out[:, depth:]
            ).astype(jnp.bfloat16)
            return carry

        lax.fori_loop(0, per, head, 0)

    def pair_copy(n):
        return pltpu.make_async_remote_copy(
            rt.at[n, pl.ds(0, tiles)], rt.at[n, pl.ds(tiles, tiles)], pair_send.at[n], pair_recv.at[n],
            device_id={"sp": partner}, device_id_type=MESH,
        )

    def goal(n):
        return wrap(n - pos[0] - pos[2])

    def part_copy(n):
        ahead = wrap(goal(n) - y)
        return pltpu.make_async_remote_copy(
            rt.at[n, pl.ds(2 * tiles, tiles)], parts.at[ahead - 1], part_send.at[n], part_recv.at[ahead - 1],
            device_id={"sp": goal(n) * 2 + c}, device_id_type=MESH,
        )

    wide_cols = min(512, width)

    def project(side, store):
        some = heads[pl.ds(pl.multiple_of(side * rows, rows), rows), :]
        for n in range(0, width, wide_cols):
            part = slice(n, min(width, n + wide_cols))
            store(part, jnp.dot(some, w[:, part], preferred_element_type=jnp.float32))

    def step(n, carry):
        chip = goal(n)
        for cc in range(2):
            t = chip * 2 + cc
            pltpu.make_async_copy(qb.at[t], qb.at[t], q_recv.at[t]).wait()
        lax.switch(chip, [functools.partial(attend, k) for k in range(chips)])

        def to_give(part, value):
            rt[n, 0:tiles, :, part] = value.astype(jnp.bfloat16).reshape(tiles, SLOTS, value.shape[1])

        def to_own(part, value):
            own[:, part] = value

        project(1 - c, to_give)
        pair_copy(n).start()
        project(c, to_own)
        pair_copy(n).wait_recv()
        both = own[...] + rt[n, tiles : 2 * tiles].reshape(rows, width).astype(jnp.float32)

        @pl.when(chip != y)
        def _():
            rt[n, 2 * tiles : 3 * tiles] = both.astype(jnp.bfloat16).reshape(tiles, SLOTS, width)
            part_copy(n).start()

        @pl.when(chip == y)
        def _():
            mine[...] = both

        return carry

    lax.fori_loop(0, chips, step, 0)

    def x_copy(a, k):
        to = device(moved(pos, a, lax.rem(pos[a] + k, line)), core)
        return pltpu.make_async_remote_copy(
            normed.at[:, cols(a)], xg.at[pos[a], :, cols(a)], x_send.at[a, k], x_recv.at[a, pos[a]],
            device_id=to, device_id_type=MESH,
        )

    hops = sorted(range(1, line), key=lambda k: (-min(k, line - k), k))

    def finish():
        total = mine[...]
        for i in range(line - 1):
            pltpu.make_async_copy(parts.at[i], parts.at[i], part_recv.at[i]).wait()
            total = total + parts[i].reshape(rows, width).astype(jnp.float32)
        attn_ref[...] = total.astype(jnp.bfloat16)
        mixed = res[...].astype(jnp.float32) + total
        power = jnp.mean(mixed * mixed, axis=1, keepdims=True)
        normed[...] = (mixed * lax.rsqrt(power + 1e-06) * gain_ref[...]).astype(jnp.bfloat16)
        for k in hops:
            for a in range(3):
                x_copy(a, k).start()
        for a in range(3):
            pltpu.make_async_copy(
                normed.at[:, cols(a)], xg.at[pos[a], :, cols(a)], x_recv.at[a, pos[a]]
            ).start()

    for a in range(3):
        for i in range(line):
            pltpu.make_async_copy(meta.at[a, i], meta.at[a, i], meta_recv.at[a, i]).wait()

    shift = line.bit_length() - 1
    q = lax.broadcasted_iota(jnp.int32, (plane, rows), 0)
    q_u = lax.shift_right_logical(q, shift + 1)
    q_v = lax.bitwise_and(lax.shift_right_logical(q, 1), line - 1)
    q_c = lax.bitwise_and(q, 1)
    big = (plane * SLOTS, plane)
    spread = jnp.where(
        lax.shift_right_logical(lax.broadcasted_iota(jnp.int32, big, 0), 4)
        == lax.broadcasted_iota(jnp.int32, big, 1),
        1.0,
        0.0,
    ).astype(jnp.bfloat16)
    slot = (
        lax.bitwise_and(lax.broadcasted_iota(jnp.int32, (plane * SLOTS, rows), 0), SLOTS - 1) + 1
    ).astype(jnp.float32)

    def routing(a, i, gated):
        u, v = others(a)
        where = [None, None, None]
        where[a], where[u], where[v] = pos[a], q_u, q_v
        expert = ((where[0] * line + where[2]) * line + where[1]) * 2 + q_c
        expert = expert.astype(jnp.float32)
        info = meta[a, i]
        place = jnp.zeros((plane, rows), jnp.float32)
        gate = jnp.zeros((plane, rows), jnp.float32)
        for k in range(8):
            match = info[k : k + 1, :] == expert
            place = place + jnp.where(match, info[8 + k : 9 + k, :], 0.0)
            if gated:
                gate = gate + jnp.where(match, info[16 + k : 17 + k, :], 0.0)
        hit = jnp.dot(spread, place.astype(jnp.bfloat16), preferred_element_type=jnp.float32) == slot
        if gated:
            value = jnp.dot(spread, gate.astype(jnp.bfloat16), preferred_element_type=jnp.float32)
        else:
            value = 1.0
        return jnp.where(hit, value, 0.0).astype(jnp.bfloat16)

    steps = [(0, 0)] + sorted(
        [(i, j) for i in range(line) for j in range(line) if (i, j) != (0, 0)],
        key=lambda o: (
            min(o[0], line - o[0]) + min(o[1], line - o[1]),
            sorted((min(o[0], line - o[0]), min(o[1], line - o[1]))),
        ),
    )

    def plane_peer(a, step, dc):
        u, v = others(a)
        p = moved(pos, u, lax.rem(pos[u] + step[0], line))
        p = moved(p, v, lax.rem(pos[v] + step[1], line))
        return p, lax.rem(core + dc, 2)

    def index_in_plane(a, p, cc):
        u, v = others(a)
        return (p[u] * line + p[v]) * 2 + cc

    def spots():
        for step in steps:
            for dc in range(2):
                for a in range(3):
                    yield a, step, dc

    group_mine = lax.rem(pos[0] + pos[1] + pos[2], line)

    def dispatch(group, carry):
        pl.when(group == group_mine)(finish)
        pair_copy(group).wait_send()

        @pl.when(goal(group) != y)
        def _():
            part_copy(group).wait_send()

        for a in range(3):
            i = source(group, a, pos)
            pltpu.make_async_copy(
                xg.at[i, :, cols(a)], xg.at[i, :, cols(a)], x_recv.at[a, i]
            ).wait()
            picked = jnp.dot(
                routing(a, i, False), xg[i, :, span(a)], preferred_element_type=jnp.float32
            ).astype(jnp.bfloat16)
            sb[group, :, :, span(a)] = picked.reshape(plane, SLOTS, columns[a][1])
        for a, step, dc in spots():
            p, cc = plane_peer(a, step, dc)
            d = moved(pos, a, source(group, a, pos))
            src = sb.at[group, index_in_plane(a, p, cc), :, cols(a)]
            dst = recv.at[group, d[0], d[2], core, :, cols(a)]
            if step == (0, 0) and dc == 0:
                pltpu.make_async_copy(src, dst, d_recv.at[group]).start()
            else:
                pltpu.make_async_remote_copy(
                    src, dst, d_send.at[a, group], d_recv.at[group],
                    device_id=device(p, cc), device_id_type=MESH,
                ).start()
        return carry

    lax.fori_loop(0, line, dispatch, 0)
    for copy in weights:
        copy.wait()

    block_ff = min(256, ff)

    def run_experts(group, carry):
        pltpu.make_async_copy(recv.at[group], recv.at[group], d_recv.at[group]).wait()

        def first(j, inner):
            x = recv[group].reshape(plane * SLOTS, width)
            at = pl.multiple_of(j * block_ff, block_ff)
            gate = jnp.dot(x, up[:, pl.ds(at, block_ff)], preferred_element_type=jnp.float32)
            lift = jnp.dot(x, up[:, pl.ds(ff + at, block_ff)], preferred_element_type=jnp.float32)
            hidden[:, pl.ds(at, block_ff)] = (
                gate / (1.0 + jnp.exp(-gate)) * lift
            ).astype(jnp.bfloat16)
            return inner

        lax.fori_loop(0, ff // block_ff, first, 0)

        def second(j, inner):
            at = pl.multiple_of(j * wide_cols, wide_cols)
            value = jnp.dot(
                hidden[...], down[:, pl.ds(at, wide_cols)], preferred_element_type=jnp.float32
            )
            recv[group, :, :, :, :, pl.ds(at, wide_cols)] = value.astype(jnp.bfloat16).reshape(
                line, line, 2, SLOTS, wide_cols
            )
            return inner

        lax.fori_loop(0, width // wide_cols, second, 0)
        for a, step, dc in spots():
            p, cc = plane_peer(a, step, dc)
            d = moved(p, a, source(group, a, p))
            src = recv.at[group, d[0], d[2], cc, :, cols(a)]
            dst = rt.at[group, index_in_plane(a, pos, core), :, cols(a)]
            if step == (0, 0) and dc == 0:
                pltpu.make_async_copy(src, dst, r_recv.at[a, group]).start()
            else:
                pltpu.make_async_remote_copy(
                    src, dst, r_send.at[a, group], r_recv.at[a, group],
                    device_id=device(p, cc), device_id_type=MESH,
                ).start()
        return carry

    lax.fori_loop(0, line, run_experts, 0)

    def s_copy(a, i):
        to = device(moved(pos, a, i), core)
        return pltpu.make_async_remote_copy(
            pb.at[i, :, cols(a)], rs.at[pos[a], :, cols(a)], s_send.at[a, i], s_recv.at[a, pos[a]],
            device_id=to, device_id_type=MESH,
        )

    def combine(group, carry):
        for a in range(3):
            i = source(group, a, pos)
            landed = rt.at[group, :, :, cols(a)]
            pltpu.make_async_copy(landed, landed, r_recv.at[a, group]).wait()
            share = lax.dot_general(
                routing(a, i, True),
                rt[group, :, :, span(a)].reshape(plane * SLOTS, columns[a][1]),
                (((0,), (0,)), ((), ())),
                preferred_element_type=jnp.float32,
            )
            pb[i, :, span(a)] = share.astype(jnp.bfloat16)

            @pl.when(i != pos[a])
            def _():
                s_copy(a, i).start()

        return carry

    lax.fori_loop(0, line, combine, 0)
    for a in range(3):
        total = pb[pos[a], :, span(a)].astype(jnp.float32)
        for k in range(1, line):
            i = lax.rem(pos[a] + k, line)
            landed = rs.at[i, :, cols(a)]
            pltpu.make_async_copy(landed, landed, s_recv.at[a, i]).wait()
            total = total + rs[i, :, span(a)].astype(jnp.float32)
        moe_ref[:, span(a)] = total.astype(jnp.bfloat16)

    for i in range(1, devices):
        k_copy(i).wait_send()
        v_copy(i).wait_send()
        l_copy(i).wait_send()
        q_copy(i).wait_send()
    for copy in cache_copies:
        copy.wait_send()
    for a in range(3):
        for k in range(1, line):
            meta_copy(a, k).wait_send()
            x_copy(a, k).wait_send()
            s_copy(a, lax.rem(pos[a] + k, line)).wait_send()
        for group in range(line):
            sent = sb.at[group, pl.ds(0, plane - 1), :, cols(a)]
            pltpu.make_async_copy(sent, sent, d_send.at[a, group]).wait()
            pltpu.make_async_copy(sent, sent, r_send.at[a, group]).wait()


def per_device(
    queries,
    fresh_key_values,
    cache,
    lengths,
    out_weight,
    residual,
    norm_gain,
    expert_ids,
    gate_values,
    up_gate_weight,
    down_weight,
):
    devices = lax.axis_size("sp")
    line = devices // 2
    rows, wide = queries.shape[0], queries.shape[1] // devices
    block, depth = cache.shape[2], cache.shape[3] // 2
    width, ff = residual.shape[1], down_weight.shape[1]
    keys = 2 * block + devices * rows
    plane = 2 * line * line
    share = width // 128
    narrow = share // 3
    cuts = [0, narrow, share - narrow, share]
    columns = [(128 * cuts[a], 128 * (cuts[a + 1] - cuts[a])) for a in range(3)]
    any_spec = pl.BlockSpec(memory_space=pl.ANY)
    vmem = pl.BlockSpec(memory_space=pltpu.VMEM)
    dma = pltpu.SemaphoreType.DMA
    half = jnp.bfloat16
    out = jax.ShapeDtypeStruct((rows, width), half)
    top = expert_ids.shape[1]
    attn_sum, mixed = pl.pallas_call(
        functools.partial(layer, line, columns),
        out_shape=(out, out),
        in_specs=[
            any_spec, any_spec, any_spec, vmem, any_spec, any_spec, vmem, vmem, vmem, any_spec, any_spec,
        ],
        out_specs=(vmem, vmem),
        scratch_shapes=[
            pltpu.VMEM((devices, rows, wide), half),
            pltpu.VMEM((keys, 2 * depth), half),
            pltpu.VMEM((keys, 2 * depth), half),
            pltpu.VMEM((devices, 8, 128), jnp.int32),
            pltpu.VMEM(out_weight.shape, half),
            pltpu.VMEM((rows, width), half),
            pltpu.VMEM((2 * rows, wide), half),
            pltpu.VMEM((rows, width), jnp.float32),
            pltpu.VMEM((rows, width), jnp.float32),
            pltpu.VMEM((line - 1, rows // SLOTS, SLOTS, width), half),
            pltpu.VMEM((rows, width), half),
            pltpu.VMEM((3 * top, rows), jnp.float32),
            pltpu.VMEM((line, rows, width), half),
            pltpu.VMEM((3, line, 3 * top, rows), jnp.float32),
            pltpu.VMEM((line, plane, SLOTS, width), half),
            pltpu.VMEM((line, line, line, 2, SLOTS, width), half),
            pltpu.VMEM((line, plane, SLOTS, width), half),
            pltpu.VMEM((line, rows, width), half),
            pltpu.VMEM((line, rows, width), half),
            pltpu.VMEM(up_gate_weight.shape[1:], half),
            pltpu.VMEM(down_weight.shape[1:], half),
            pltpu.VMEM((plane * SLOTS, ff), half),
            dma((devices,)), dma((devices,)), dma((devices,)), dma((devices,)),
            dma((devices,)), dma((devices,)), dma((devices,)), dma((devices,)),
            dma((2,)), dma((2,)), dma((7,)), dma((line,)), dma((line,)), dma((line,)), dma((line,)),
            dma((2,)),
            dma((3, line)), dma((3, line)), dma((3, line)), dma((3, line)),
            dma((3, line)), dma((line,)), dma((3, line)), dma((3, line)),
            dma((3, line)), dma((3, line)),
        ],
        compiler_params=pltpu.CompilerParams(
            collective_id=0, has_side_effects=True, vmem_limit_bytes=67_000_000
        ),
    )(
        queries,
        fresh_key_values,
        cache[0, 0],
        jnp.broadcast_to(lengths, (8, 128)),
        out_weight,
        residual,
        norm_gain[None, :],
        expert_ids.T,
        gate_values.T,
        up_gate_weight,
        down_weight,
    )
    own_live = (jnp.arange(rows, dtype=jnp.int32) < lengths[0, 0])[:, None]
    zero = jnp.zeros((), half)
    return (jnp.where(own_live, attn_sum, zero), jnp.where(own_live, mixed, zero))


def solution(mesh):
    in_specs = (
        P(("grp", "sp"), None),
        P(("grp", "sp"), None),
        P("grp", "sp", None, None),
        P("grp", "sp"),
        P("sp", None),
        P(("grp", "sp"), None),
        P(),
        P(("grp", "sp"), None),
        P(("grp", "sp"), None),
        P(("grp", "sp"), None, None),
        P(("grp", "sp"), None, None),
    )
    out_specs = (P(("grp", "sp"), None), P(("grp", "sp"), None))
    return jax.shard_map(
        per_device, mesh=mesh, in_specs=in_specs, out_specs=out_specs, check_vma=False
    )
```

time: 240 us -> 268 us (1.12)
  Pallas kernels: 228 us -> 263 us
  local copies, waits for them, and re-layouts: 5.41 us -> 0.6 us
    pallas_call x2 -> x1, Pallas kernels: 228 us -> 263 us  [per_device(): pl.pallas_call(functools.partial(layer, line, columns), out_shape=(out, o...]
    unnamed x3 -> x0, local copies, waits for them, and re-layouts: 4.76 us -> none
where the time goes in v3:
time: 268 us; the launch traced here: 267 us
  Pallas kernels  263 us (98%)
    pallas_call x1, Pallas kernels, per_device(): pl.pallas_call(functools.partial(layer, line, columns), out_shape=(out, o...  263 us

profile of v3, /device:TPU:1, one launch (start us, length us, event | category | flops | bytes accessed | tf_op | source)
XLA Modules:
  0.0 266.9 jit_solution(16157665427662364057)
XLA Ops:
  1.3 0.6 broadcast_in_dim.26.lens_ref
  1.9 262.5 %shard_map.122 = (bf16[160,2048]{1,0:T(8,128)(2,1)}, bf16[160,2048]{1,0:T(8,128)(2,1)}) custom-call(bf16[160,4096]{1,0:T(8,128)(2,1)} %q_hbm.1, bf16[160,1024]{1,0:T(8,128)(2,1)} %fkv_hbm.1, bf16[256,256]{1,0:T(8,128)(2,1)} %bitcast.7, s32[8,128]{1,0:T(8,128)} %broadcast_in_dim.26.lens_ref, bf16[512,2048]{1,0:T(8,128)(2,1)} %w_hbm.1, ...), custom_call_target="tpu_custom_call" | custom-call | tf_op jit(solution)/shard_map/pallas_call | solution.py:561
  264.4 2.5 broadcast_select_fusion
  (1 shorter events, 0.0 us)

commit v4 on v2

--- a/solution.py
+++ b/solution.py
@@ -14,8 +14,9 @@
 
 
 def group_attention(
-    q_hbm, fkv_hbm, cache_hbm, lens_ref, w_hbm, res_hbm, gain_ref,
-    attended_ref, normed_ref,
+    experts,
+    q_hbm, fkv_hbm, cache_hbm, lens_ref, w_hbm, res_hbm, gain_ref, ids_ref, gates_ref,
+    attended_ref, normed_ref, info,
     qb, kx, vx, lb, w, res, heads, own_part, give, take, relay, half_in, full_in,
     q_send, k_send, v_send, l_send, q_recv, k_recv, v_recv, l_recv,
     c_send, c_recv, local, pair_send, pair_recv, ring_send, ring_recv,
@@ -122,6 +123,26 @@
         for cc in range(2):
             q_copy(lax.rem(y + dy, chips) * 2 + cc).start()
 
+    lanes = lax.broadcasted_iota(jnp.int32, (8, rows), 1)
+    living = lanes < lens_ref[:, 0:1]
+    expert_rows = lax.broadcasted_iota(jnp.int32, (experts, rows), 0)
+    named = jnp.where(living, ids_ref[...], experts)
+    routed = jnp.zeros((experts, rows), jnp.float32)
+    for k in range(8):
+        routed = routed + jnp.where(named[k : k + 1, :] == expert_rows, 1.0, 0.0)
+    square = (rows, rows)
+    before = jnp.where(
+        lax.broadcasted_iota(jnp.int32, square, 0) < lax.broadcasted_iota(jnp.int32, square, 1),
+        1.0,
+        0.0,
+    ).astype(jnp.bfloat16)
+    prefix = jnp.dot(routed.astype(jnp.bfloat16), before, preferred_element_type=jnp.float32)
+    info[0:8, :] = named.astype(jnp.float32)
+    for k in range(8):
+        hits = jnp.where(named[k : k + 1, :] == expert_rows, prefix, 0.0)
+        info[8 + k : 9 + k, :] = jnp.sum(hits, axis=0, keepdims=True) + 1.0
+    info[16:24, :] = gates_ref[...]
+
     for copy in local_copies:
         copy.wait()
     for copy in cache_copies:
@@ -267,9 +288,7 @@
     own_part[0] = own_part[0] + full_in[0].astype(jnp.float32)
     ring_copy(3).wait_recv()
     total = own_part[0] + full_in[1].astype(jnp.float32)
-    alive = lax.broadcasted_iota(jnp.int32, (rows, 128), 0) < lens_ref[0:1, :]
-    keep = jnp.max(jnp.where(alive, 1.0, 0.0), axis=1, keepdims=True)
-    attended_ref[...] = jnp.where(keep > 0.0, total, 0.0).astype(jnp.bfloat16)
+    attended_ref[...] = total.astype(jnp.bfloat16)
     mixed = res[...].astype(jnp.float32) + total
     power = jnp.mean(mixed * mixed, axis=1, keepdims=True)
     normed_ref[...] = (mixed * lax.rsqrt(power + 1e-06) * gain_ref[...]).astype(jnp.bfloat16)
@@ -286,7 +305,11 @@
         ring_copy(n).wait_send()
 
 
-def attention(queries, fresh_key_values, cache, lengths, out_weight, residual, norm_gain):
+def attention(
+    queries, fresh_key_values, cache, lengths, out_weight, residual, norm_gain, expert_ids, gate_values
+):
+    experts = lax.axis_size("grp") * lax.axis_size("sp")
+    top = expert_ids.shape[1]
     devices = lax.axis_size("sp")
     rows, wide = queries.shape[0], queries.shape[1] // devices
     block, depth = cache.shape[2], cache.shape[3] // 2
@@ -297,10 +320,10 @@
     dma = pltpu.SemaphoreType.DMA
     out = jax.ShapeDtypeStruct((rows, width), jnp.bfloat16)
     return pl.pallas_call(
-        group_attention,
-        out_shape=(out, out),
-        in_specs=[any_spec, any_spec, any_spec, vmem, any_spec, any_spec, vmem],
-        out_specs=(vmem, vmem),
+        functools.partial(group_attention, experts),
+        out_shape=(out, out, jax.ShapeDtypeStruct((3 * top, rows), jnp.float32)),
+        in_specs=[any_spec, any_spec, any_spec, vmem, any_spec, any_spec, vmem, vmem, vmem],
+        out_specs=(vmem, vmem, vmem),
         scratch_shapes=[
             pltpu.VMEM((devices, rows, wide), jnp.bfloat16),
             pltpu.VMEM((keys, 2 * depth), jnp.bfloat16),
@@ -330,6 +353,8 @@
         out_weight,
         residual,
         norm_gain[None, :],
+        expert_ids.T,
+        gate_values.T,
     )
 
 
@@ -340,12 +365,14 @@
     line, columns,
     normed_hbm, meta_hbm, up_hbm, down_hbm,
     out_ref,
-    xg0, xg1, xg2, meta, sb0, sb1, sb2, recv, ready, rt0, rt1, rt2,
+    xg0, xg1, xg2, meta, sb0, sb1, sb2, rc0, rc1, rc2, rd0, rd1, rd2, rt0, rt1, rt2,
     rs0, rs1, rs2, pb0, pb1, pb2, up, down, hidden,
     w_sem, meta_send, meta_recv, x_send, x_recv, d_send, d_recv,
     r_send, r_recv, s_send, s_recv,
 ):
-    xg, sb, rt, rs, pb = (xg0, xg1, xg2), (sb0, sb1, sb2), (rt0, rt1, rt2), (rs0, rs1, rs2), (pb0, pb1, pb2)
+    xg, sb, rt = (xg0, xg1, xg2), (sb0, sb1, sb2), (rt0, rt1, rt2)
+    rs, pb = (rs0, rs1, rs2), (pb0, pb1, pb2)
+    recv, ready = (rc0, rc1, rc2), (rd0, rd1, rd2)
     grp, sp = lax.axis_index("grp"), lax.axis_index("sp")
     pos = (grp // line, sp // 2, lax.rem(grp, line))
     core = lax.rem(sp, 2)
@@ -373,6 +400,9 @@
 
     def cols(a):
         return pl.ds(columns[a][0], columns[a][1])
+
+    def span(a):
+        return slice(columns[a][0], columns[a][0] + columns[a][1])
 
     bar = pltpu.get_barrier_semaphore()
     peers = [
@@ -416,9 +446,14 @@
     for k in hops:
         for a in range(3):
             meta_copy(a, k).start()
-    for k in hops:
-        for a in range(3):
-            x_copy(a, k).start()
+
+    def share_rows():
+        for k in hops:
+            for a in range(3):
+                x_copy(a, k).start()
+
+    group_mine = lax.rem(pos[0] + pos[1] + pos[2], line)
+    share_rows()
     for a in range(3):
         for i in range(line):
             pltpu.make_async_copy(meta.at[a, i], meta.at[a, i], meta_recv.at[a, i]).wait()
@@ -479,29 +514,31 @@
         return (p[u] * line + p[v]) * 2 + cc
 
     def spots():
-        for step in steps:
-            for dc in range(2):
+        for dc in range(2):
+            for step in steps:
                 for a in range(3):
                     yield a, step, dc
 
     def dispatch(group, carry):
+
+        chosen = [routing(a, source(group, a, pos), False) for a in range(3)]
         for a in range(3):
             i = source(group, a, pos)
             pltpu.make_async_copy(xg[a].at[i], xg[a].at[i], x_recv.at[a, i]).wait()
             picked = jnp.dot(
-                routing(a, i, False), xg[a][i], preferred_element_type=jnp.float32
+                chosen[a], xg[a][i], preferred_element_type=jnp.float32
             ).astype(jnp.bfloat16)
             sb[a][group] = picked.reshape(plane, SLOTS, columns[a][1])
         for a, step, dc in spots():
             p, cc = plane_peer(a, step, dc)
             d = moved(pos, a, source(group, a, pos))
             src = sb[a].at[group, index_in_plane(a, p, cc)]
-            dst = recv.at[group, d[0], d[2], core, :, cols(a)]
+            dst = recv[a].at[group, d[0], d[2], core]
             if step == (0, 0) and dc == 0:
-                pltpu.make_async_copy(src, dst, d_recv.at[group]).start()
+                pltpu.make_async_copy(src, dst, d_recv.at[a, group]).start()
             else:
                 pltpu.make_async_remote_copy(
-                    src, dst, d_send.at[a, group], d_recv.at[group],
+                    src, dst, d_send.at[a, group], d_recv.at[a, group],
                     device_id=device(p, cc), device_id_type=MESH,
                 ).start()
         return carry
@@ -511,13 +548,16 @@
         copy.wait()
 
     block = min(256, ff)
-    wide = min(512, width)
 
     def experts(group, carry):
-        pltpu.make_async_copy(recv.at[group], recv.at[group], d_recv.at[group]).wait()
+        for a in range(3):
+            landed = recv[a].at[group]
+            pltpu.make_async_copy(landed, landed, d_recv.at[a, group]).wait()
 
         def first(j, inner):
-            x = recv[group].reshape(plane * SLOTS, width)
+            x = jnp.concatenate(
+                [recv[a][group].reshape(plane * SLOTS, columns[a][1]) for a in range(3)], axis=1
+            )
             at = pl.multiple_of(j * block, block)
             gate = jnp.dot(x, up[:, pl.ds(at, block)], preferred_element_type=jnp.float32)
             lift = jnp.dot(x, up[:, pl.ds(ff + at, block)], preferred_element_type=jnp.float32)
@@ -526,21 +566,15 @@
 
         lax.fori_loop(0, ff // block, first, 0)
 
-        def second(j, inner):
-            at = pl.multiple_of(j * wide, wide)
-            value = jnp.dot(
-                hidden[...], down[:, pl.ds(at, wide)], preferred_element_type=jnp.float32
+        for a in range(3):
+            value = jnp.dot(hidden[...], down[:, span(a)], preferred_element_type=jnp.float32)
+            ready[a][group] = value.astype(jnp.bfloat16).reshape(
+                line, line, 2, SLOTS, columns[a][1]
             )
-            ready[group, :, :, :, :, pl.ds(at, wide)] = value.astype(jnp.bfloat16).reshape(
-                line, line, 2, SLOTS, wide
-            )
-            return inner
-
-        lax.fori_loop(0, width // wide, second, 0)
         for a, step, dc in spots():
             p, cc = plane_peer(a, step, dc)
             d = moved(p, a, source(group, a, p))
-            src = ready.at[group, d[0], d[2], cc, :, cols(a)]
+            src = ready[a].at[group, d[0], d[2], cc]
             dst = rt[a].at[group, index_in_plane(a, pos, core)]
             if step == (0, 0) and dc == 0:
                 pltpu.make_async_copy(src, dst, r_recv.at[a, group]).start()
@@ -563,9 +597,10 @@
     def combine(group, carry):
         for a in range(3):
             i = source(group, a, pos)
+            mixing = routing(a, i, True)
             pltpu.make_async_copy(rt[a].at[group], rt[a].at[group], r_recv.at[a, group]).wait()
             share = lax.dot_general(
-                routing(a, i, True),
+                mixing,
                 rt[a][group].reshape(plane * SLOTS, columns[a][1]),
                 (((0,), (0,)), ((), ())),
                 preferred_element_type=jnp.float32,
@@ -613,7 +648,6 @@
     def buffers(*shape):
         return [pltpu.VMEM((*shape, columns[a][1]), jnp.bfloat16) for a in range(3)]
 
-    whole = pltpu.VMEM((line, line, line, 2, SLOTS, width), jnp.bfloat16)
     return pl.pallas_call(
         functools.partial(expert_exchange, line, columns),
         out_shape=jax.ShapeDtypeStruct((rows, width), jnp.bfloat16),
@@ -623,8 +657,8 @@
             *buffers(line, rows),
             pltpu.VMEM((3, line, *meta.shape), jnp.float32),
             *buffers(line, plane, SLOTS),
-            whole,
-            whole,
+            *buffers(line, line, line, 2, SLOTS),
+            *buffers(line, line, line, 2, SLOTS),
             *buffers(line, plane, SLOTS),
             *buffers(line, rows),
             *buffers(line, rows),
@@ -633,7 +667,7 @@
             pltpu.VMEM((plane * SLOTS, ff), jnp.bfloat16),
             dma((2,)),
             dma((3, line)), dma((3, line)), dma((3, line)), dma((3, line)),
-            dma((3, line)), dma((line,)), dma((3, line)), dma((3, line)),
+            dma((3, line)), dma((3, line)), dma((3, line)), dma((3, line)),
             dma((3, line)), dma((3, line)),
         ],
         compiler_params=pltpu.CompilerParams(
@@ -657,19 +691,14 @@
 ):
     seq_devices = lax.axis_size("sp")
     slot_rows = queries.shape[0]
-    attended, normed = attention(
-        queries, fresh_key_values, cache, lengths, out_weight, residual, norm_gain
+    attn_sum, normed, info = attention(
+        queries, fresh_key_values, cache, lengths, out_weight, residual, norm_gain, expert_ids, gate_values
     )
-    own_live = jnp.arange(slot_rows, dtype=jnp.int32) < lengths[0, 0]
-    experts = up_gate_weight.shape[0] * lax.axis_size("grp") * lax.axis_size("sp")
-    choose = expert_ids[:, :, None] == jnp.arange(experts, dtype=jnp.int32)[None, None, :]
-    routed = (jnp.any(choose, axis=1) & own_live[:, None]).astype(jnp.float32)
-    earlier = (jnp.arange(slot_rows)[:, None] > jnp.arange(slot_rows)[None, :]).astype(jnp.float32)
-    prefix = jnp.dot(earlier, routed, precision=lax.Precision.HIGHEST)
-    slot_in = jnp.sum(jnp.where(choose, prefix[:, None, :], 0.0), axis=2)
-    chosen = jnp.where(own_live[:, None], expert_ids, experts).astype(jnp.float32)
-    meta = jnp.concatenate([chosen, slot_in + 1.0, gate_values], axis=1).T
-    return (attended, mix_experts(normed, meta, up_gate_weight, down_weight))
+    mixed = mix_experts(normed, info, up_gate_weight, down_weight)
+    slots = jnp.arange(queries.shape[0], dtype=jnp.int32)
+    own_live = (slots < lengths[0, 0])[:, None]
+    zero = jnp.zeros((), jnp.bfloat16)
+    return (jnp.where(own_live, attn_sum, zero), jnp.where(own_live, mixed, zero))
 
 
 def solution(mesh):

time: 240 us -> 232 us (0.967)
  local copies, waits for them, and re-layouts: 5.41 us -> 0.6 us
    unnamed x3 -> x0, local copies, waits for them, and re-layouts: 4.76 us -> none
    select_n x0 -> x1, other arithmetic: none -> 2.5 us  [per_device(): jnp.where(own_live, mixed, zero)]
where the time goes in v4:
time: 232 us
  Pallas kernels  227 us (98%)
  other arithmetic  2.5 us (1%)
    pallas_call x1, Pallas kernels, mix_experts(): pl.pallas_call(functools.partial(expert_exchange, line, columns), out_sha...  163 us
    pallas_call x1, Pallas kernels, attention(): pl.pallas_call(functools.partial(group_attention, experts), out_shape=(ou...  64.4 us

profile of v4, /device:TPU:1, one launch (start us, length us, event | category | flops | bytes accessed | tf_op | source)
XLA Modules:
  0.0 231.8 jit_solution(10034262835749624901)
XLA Ops:
  1.3 0.6 broadcast_in_dim.26.lens_ref
  1.9 64.4 %shard_map.122 = (bf16[160,2048]{1,0:T(8,128)(2,1)}, bf16[160,2048]{1,0:T(8,128)(2,1)}, f32[24,160]{1,0:T(8,128)}) custom-call(bf16[160,4096]{1,0:T(8,128)(2,1)} %q_hbm.1, bf16[160,1024]{1,0:T(8,128)(2,1)} %fkv_hbm.1, bf16[256,256]{1,0:T(8,128)(2,1)} %bitcast.7, s32[8,128]{1,0:T(8,128)} %broadcast_in_dim.26.lens_ref, bf16[512,2048]{1,0:T(8,128)(2,1)} %w_hbm.1, ...), custom_call_target="tpu_custom_call" | custom-call | tf_op jit(solution)/shard_map/pallas_call | solution.py:322
  66.3 163.0 %shard_map.123 = bf16[160,2048]{1,0:T(8,128)(2,1)} custom-call(bf16[160,2048]{1,0:T(8,128)(2,1)} %get-tuple-element.6.normed_hbm, f32[24,160]{1,0:T(8,128)} %get-tuple-element.7.meta_hbm, bf16[1,2048,1536]{2,1,0:T(8,128)(2,1)} %up_hbm.1, bf16[1,768,2048]{2,1,0:T(8,128)(2,1)} %down_hbm.1), custom_call_target="tpu_custom_call" | custom-call | tf_op jit(solution)/shard_map/pallas_call | solution.py:651
  229.3 2.5 %broadcast_select_fusion = (bf16[160,2048]{1,0:T(8,128)(2,1)}, bf16[160,2048]{1,0:T(8,128)(2,1)}) fusion(bf16[160,2048]{1,0:T(8,128)(2,1)} %shard_map.123, pred[160]{0:T(512)(128)(4,1)S(1)} %iota_compare_fusion, bf16[160,2048]{1,0:T(8,128)(2,1)} %get-tuple-element.5), kind=kLoop, calls=%fused_computation | loop fusion | flops 655360 | bytes 2621600 | tf_op jit(solution)/shard_map/jit(_where)/select_n | solution.py:701
  (1 shorter events, 0.0 us)

commit v5 on v4

--- a/solution.py
+++ b/solution.py
@@ -119,9 +119,9 @@
     for copy in cache_copies:
         copy.start()
     q_copy(partner).start()
-    for dy in (2, 1, 3):
-        for cc in range(2):
-            q_copy(lax.rem(y + dy, chips) * 2 + cc).start()
+    for dc in range(2):
+        for dy in (2, 1, 3):
+            q_copy(lax.rem(y + dy, chips) * 2 + lax.rem(c + dc, 2)).start()
 
     lanes = lax.broadcasted_iota(jnp.int32, (8, rows), 1)
     living = lanes < lens_ref[:, 0:1]

time: 232 us -> 236 us (1.017)
  Pallas kernels: 227 us -> 230 us
    pallas_call x1, Pallas kernels: 64.4 us -> 67.7 us  [attention(): pl.pallas_call(functools.partial(group_attention, experts), out_shape=(ou...]
where the time goes in v5:
time: 236 us; the launch traced here: 234 us
  Pallas kernels  230 us (97%)
  other arithmetic  2.5 us (1%)
    pallas_call x1, Pallas kernels, mix_experts(): pl.pallas_call(functools.partial(expert_exchange, line, columns), out_sha...  162 us
    pallas_call x1, Pallas kernels, attention(): pl.pallas_call(functools.partial(group_attention, experts), out_shape=(ou...  67.7 us

profile of v5, /device:TPU:1, one launch (start us, length us, event | category | flops | bytes accessed | tf_op | source)
XLA Modules:
  0.0 233.9 jit_solution(11394219071568269892)
XLA Ops:
  1.3 0.6 broadcast_in_dim.26.lens_ref
  1.9 67.7 %shard_map.122 = (bf16[160,2048]{1,0:T(8,128)(2,1)}, bf16[160,2048]{1,0:T(8,128)(2,1)}, f32[24,160]{1,0:T(8,128)}) custom-call(bf16[160,4096]{1,0:T(8,128)(2,1)} %q_hbm.1, bf16[160,1024]{1,0:T(8,128)(2,1)} %fkv_hbm.1, bf16[256,256]{1,0:T(8,128)(2,1)} %bitcast.7, s32[8,128]{1,0:T(8,128)} %broadcast_in_dim.26.lens_ref, bf16[512,2048]{1,0:T(8,128)(2,1)} %w_hbm.1, ...), custom_call_target="tpu_custom_call" | custom-call | tf_op jit(solution)/shard_map/pallas_call | solution.py:322
  69.6 161.8 %shard_map.123 = bf16[160,2048]{1,0:T(8,128)(2,1)} custom-call(bf16[160,2048]{1,0:T(8,128)(2,1)} %get-tuple-element.6.normed_hbm, f32[24,160]{1,0:T(8,128)} %get-tuple-element.7.meta_hbm, bf16[1,2048,1536]{2,1,0:T(8,128)(2,1)} %up_hbm.1, bf16[1,768,2048]{2,1,0:T(8,128)(2,1)} %down_hbm.1), custom_call_target="tpu_custom_call" | custom-call | tf_op jit(solution)/shard_map/pallas_call | solution.py:651
  231.4 2.5 %broadcast_select_fusion = (bf16[160,2048]{1,0:T(8,128)(2,1)}, bf16[160,2048]{1,0:T(8,128)(2,1)}) fusion(bf16[160,2048]{1,0:T(8,128)(2,1)} %shard_map.123, pred[160]{0:T(512)(128)(4,1)S(1)} %iota_compare_fusion, bf16[160,2048]{1,0:T(8,128)(2,1)} %get-tuple-element.5), kind=kLoop, calls=%fused_computation | loop fusion | flops 655360 | bytes 2621600 | tf_op jit(solution)/shard_map/jit(_where)/select_n | solution.py:701
  (1 shorter events, 0.0 us)
